TPU v7x, 768 devices: a whole 4x8x12 slice. The times are simulated.
768 devices in a mesh: seq: 48 (over y_hi, z, core), fsdp: 4 (over x), batch: 4 (over y_lo).
Axes of the slice: x: 4, y: 8 (y_hi: 2, y_lo: 4; y = y_hi * 4 + y_lo), z: 12, core: 2. Of those that a mesh axis runs over, the one named last changes fastest.
Arguments:
- hidden: bfloat16 [16, 6144, 2048], P(('fsdp', 'batch'), 'seq'), may hold values from -6 to 6
- in_weight: bfloat16 [2048, 2208], P(('fsdp', 'batch')), may hold values from -0.125 to 0.125
- read_starts: int32 [16, 4], P(('fsdp', 'batch')), may hold values from 1 to 6143
- conv_weight: float32 [2, 4, 2176], replicated, may hold values from -3 to 3
- conv_bias: float32 [2, 2176], replicated, may hold values from -0.5 to 0.5
- dt_bias: float32 [2, 32], replicated, may hold values from -4.5 to -2.5
- decay: float32 [2, 32], replicated, may hold values from 8.138021e-06 to 0.7
- skip: float32 [2, 32], replicated, may hold values from 0.5 to 1.5
- norm_gain: float32 [2, 2048], replicated, may hold values from 0.5 to 1.5
Outputs:
- mixed: bfloat16 [16, 6144, 2048], P(('fsdp', 'batch'), 'seq')
All inputs are finite; a program needn't handle non-finite values.
Results may differ from a plain program's by a relative error of at most 0.0051.
Values may be sent and summed in bfloat16 or wider, within the bound.
A program may use at most 128 MiB of HBM per device.

v0:
```python
import jax
import jax.numpy as jnp
from jax import lax
from jax.sharding import PartitionSpec as P

HEADS = 32
HEAD_DIM = 64
STATE = 64
KERNEL = 4
BLOCK = 128
INNER = 2048
CONV_CH = 2176


def prefix(value, axis, join, neutral, backward):
    count, mine = (lax.axis_size(axis), lax.axis_index(axis))
    pieces = jax.tree.map(lambda part: lax.all_gather(part, axis), value)
    if backward:
        pieces = jax.tree.map(lambda part: part[::-1], pieces)
        mine = count - 1 - mine
    running = jax.tree.map(
        lambda part, zero: jnp.full_like(part, 0) + jnp.asarray(zero, part.dtype), value, neutral
    )

    def turn(position, running):
        longer = join(running, jax.tree.map(lambda part: part[position], pieces))
        return jax.tree.map(lambda new, old: jnp.where(position < mine, new, old), longer, running)

    return lax.fori_loop(0, count - 1, turn, running)


def extended_2(value, sides, width):
    for axis, dim in sides:
        size, length = (lax.axis_size(axis), value.shape[dim])
        up = [(i, (i + 1) % size) for i in range(size - 1)]
        down = [(j, i) for i, j in up]
        last = lax.slice_in_dim(value, length - width, length, axis=dim)
        initial = lax.slice_in_dim(value, 0, width, axis=dim)
        before = lax.ppermute(last, axis, up)
        after = lax.ppermute(initial, axis, down)
        value = jnp.concatenate([before, value, after], axis=dim)
    return value


def conv_silu(padded, weight, bias):
    length = padded.shape[0] - weight.shape[0] + 1
    total = jnp.broadcast_to(bias[None, :], (length, bias.shape[0]))
    for tap in range(weight.shape[0]):
        total = total + weight[tap][None, :] * padded[tap : tap + length].astype(jnp.float32)
    return jax.nn.silu(total).astype(jnp.bfloat16)


def block_parts(x_part, b_part, c_part, step_size, log_rate, resets):
    length = x_part.shape[0]
    running = jnp.cumsum(log_rate, axis=0)
    running_heads = running.T
    step_heads = step_size.T
    resets_seen = jnp.cumsum(resets)
    scores = jnp.dot(c_part, b_part.T, preferred_element_type=jnp.float32)
    positions = jnp.arange(length)
    allowed = (positions[:, None] >= positions[None, :]) & (
        resets_seen[:, None] == resets_seen[None, :]
    )
    log_gaps = jnp.minimum(running_heads[:, :, None] - running_heads[:, None, :], 0.0)
    weights = (
        jnp.where(allowed[None, :, :], jnp.exp(log_gaps), 0.0)
        * scores[None, :, :]
        * step_heads[:, None, :]
    )
    weights = weights.astype(jnp.bfloat16)
    values = x_part.reshape(length, HEADS, HEAD_DIM)
    inner_part = jnp.einsum("hts,shp->thp", weights, values, preferred_element_type=jnp.float32)
    last_same = resets_seen == resets_seen[-1]
    tail_weight = (
        jnp.where(last_same[:, None], jnp.exp(running[-1][None, :] - running), 0.0) * step_size
    )
    inputs = (tail_weight[:, :, None] * values.astype(jnp.float32)).astype(jnp.bfloat16)
    local_end = jnp.einsum("shp,sn->hpn", inputs, b_part, preferred_element_type=jnp.float32)
    lead_fade = jnp.where((resets_seen == 0)[:, None], jnp.exp(running), 0.0)
    block_fade = jnp.where(resets_seen[-1] == 0, jnp.exp(running[-1]), 0.0)
    return (inner_part, local_end, lead_fade, block_fade)


def chain_combine(earlier, later):
    return (earlier[0] * later[0], later[0][:, None] * earlier[1] + later[1])


def direction(conv_out, step_cols, resets, bias_step, rates, direct, gains, backward):
    length = conv_out.shape[0]
    blocks = length // BLOCK
    x_part = conv_out[:, :INNER]
    b_part = conv_out[:, INNER : INNER + STATE]
    c_part = conv_out[:, INNER + STATE :]
    step_size = jax.nn.softplus(step_cols.astype(jnp.float32) + bias_step[None, :])
    log_rate = -step_size * rates[None, :]
    inner_part, local_end, lead_fade, block_fade = jax.vmap(block_parts)(
        x_part.reshape(blocks, BLOCK, INNER),
        b_part.reshape(blocks, BLOCK, STATE),
        c_part.reshape(blocks, BLOCK, STATE),
        step_size.reshape(blocks, BLOCK, HEADS),
        log_rate.reshape(blocks, BLOCK, HEADS),
        resets.reshape(blocks, BLOCK),
    )
    carried_state = jnp.zeros((HEADS, HEAD_DIM, STATE), jnp.float32)
    carried_fade = jnp.ones((HEADS,), jnp.float32)
    entering = carried_state
    fades_before = carried_fade
    carried_state = block_fade[0][:, None, None] * carried_state + local_end[0]
    carried_fade = block_fade[0] * carried_fade
    summary = (carried_fade, carried_state.reshape(HEADS, HEAD_DIM * STATE))
    identity = (jnp.ones((HEADS,), jnp.float32), jnp.zeros((HEADS, HEAD_DIM * STATE), jnp.float32))
    if backward:
        incoming = prefix(summary, "seq", chain_combine, identity, True)
    else:
        incoming = prefix(summary, "seq", chain_combine, identity, False)
    incoming_state = incoming[1].reshape(HEADS, HEAD_DIM, STATE)
    states = jnp.stack([fades_before[:, None, None] * incoming_state + entering])
    rounded = states.astype(jnp.bfloat16)
    carried = jnp.einsum(
        "btn,bhpn->bthp",
        c_part.reshape(blocks, BLOCK, STATE),
        rounded,
        preferred_element_type=jnp.float32,
    )
    direct_part = direct[None, None, :, None] * x_part.reshape(
        blocks, BLOCK, HEADS, HEAD_DIM
    ).astype(jnp.float32)
    result = (inner_part + lead_fade[..., None] * carried + direct_part).reshape(
        length, HEADS, HEAD_DIM
    )
    scale = lax.rsqrt(jnp.mean(result * result, axis=-1, keepdims=True) + 1e-05)
    return (result * scale * gains.reshape(HEADS, HEAD_DIM)).reshape(length, INNER)


def project(rows_in, in_weight):
    total = jnp.dot(
        rows_in,
        lax.all_gather(in_weight, ("fsdp", "batch"), axis=0, tiled=True),
        preferred_element_type=jnp.float32,
    )
    return total.astype(jnp.bfloat16)


def on_device(
    hidden, in_weight, read_starts, conv_weight, conv_bias, dt_bias, decay, skip, norm_gain
):
    tokens = hidden[0]
    length = tokens.shape[0]
    margin = KERNEL - 1
    projected = project(tokens, in_weight)
    extended = extended_2(projected[:, :CONV_CH], (("seq", 0),), margin)
    forward_in = conv_silu(extended[: length + margin], conv_weight[0], conv_bias[0])
    backward_in = conv_silu(jnp.flip(extended[margin:], 0), conv_weight[1], conv_bias[1])
    step_cols = projected[:, CONV_CH:]
    positions = lax.axis_index("seq") * length + jnp.arange(length, dtype=jnp.int32)
    marks = read_starts[0]
    starts_here = jnp.any(positions[:, None] == marks[None, :], axis=1).astype(jnp.float32)
    starts_next = jnp.any((positions + 1)[:, None] == marks[None, :], axis=1).astype(jnp.float32)
    forward_out = direction(
        forward_in, step_cols, starts_here, dt_bias[0], decay[0], skip[0], norm_gain[0], False
    )
    backward_out = direction(
        backward_in,
        jnp.flip(step_cols, 0),
        jnp.flip(starts_next, 0),
        dt_bias[1],
        decay[1],
        skip[1],
        norm_gain[1],
        True,
    )
    mixed = forward_out + jnp.flip(backward_out, 0)
    return mixed.astype(jnp.bfloat16)[None]


def solution(mesh):
    in_specs = (
        P(("fsdp", "batch"), "seq", None),
        P(("fsdp", "batch"), None),
        P(("fsdp", "batch"), None),
        P(),
        P(),
        P(),
        P(),
        P(),
        P(),
    )
    out_specs = P(("fsdp", "batch"), "seq", None)
    return jax.shard_map(
        on_device, mesh=mesh, in_specs=in_specs, out_specs=out_specs, check_vma=False
    )
```

profile of v0, /device:TPU:1, one launch (start us, length us, event | category | flops | bytes accessed | tf_op | source)
XLA Modules:
  0.0 899.9 jit_solution(16220850641270696242)
XLA Ops:
  13.8 207.0 %all-gather.6.cloned.1.call-done = bf16[2048,2208]{0,1:T(8,128)(2,1)} async-done(((bf16[128,2208]{0,1:T(8,128)(2,1)}), bf16[2048,2208]{0,1:T(8,128)(2,1)}) %all-gather.6.cloned.1.call-update) | async-done | bytes 9043984 | tf_op jit(solution)/shard_map/all_gather | solution.py:138
  220.8 6.1 convolution_convert_fusion
  228.8 3.4 collective-permute-start
  233.4 2.6 multiply_convert_fusion.3
  242.6 1.9 collective-permute-start.1
  245.2 1.6 slice.189
  247.5 75.8 %all-gather.1 = f32[48,1,32]{2,1,0:T(1,128)S(1)} all-gather(f32[1,1,32]{2,1,0:T(1,128)S(1)} %get-tuple-element.277), channel_id=3, replica_groups=mesh['seq'=48,'fsdp'=4,'batch'=4] {'seq'}, dimensions={0}, use_global_device_ids=true | all-gather | bytes 6272 | tf_op jit(solution)/shard_map/all_gather | solution.py:17
  324.0 72.0 %all-gather = f32[48,1,32]{2,1,0:T(1,128)} all-gather(f32[1,1,32]{2,1,0:T(1,128)S(1)} %get-tuple-element.275), channel_id=2, replica_groups=mesh['seq'=48,'fsdp'=4,'batch'=4] {'seq'}, dimensions={0}, use_global_device_ids=true | all-gather | bytes 6272 | tf_op jit(solution)/shard_map/all_gather | solution.py:17
  396.3 2.2 fusion.27
  398.5 7.7 slice.181
  406.2 8.9 slice.184
  415.1 6.1 slice.187
  421.2 3.5 multiply_convert_fusion.2
  427.9 1.3 slice_convert_fusion.1
  431.2 95.9 %all-gather.8.cloned.1.call-done = f32[48,32,4096]{2,1,0:T(8,128)} async-done(((f32[1,32,4096]{2,1,0:T(8,128)}), f32[48,32,4096]{2,1,0:T(8,128)}) %all-gather.8.cloned.1.call-update) | async-done | bytes 25165840 | tf_op jit(solution)/shard_map/all_gather | solution.py:17
  527.1 88.3 %while.28 = (s32[]{:T(128)}, f32[32,4096]{1,0:T(8,128)S(1)}, s32[]{:T(128)}, f32[48,32]{1,0:T(8,128)}, f32[48,32,4096]{2,1,0:T(8,128)}, /*index=5*/s32[]{:T(128)}, s32[]{:T(128)}) while((s32[]{:T(128)}, f32[32,4096]{1,0:T(8,128)S(1)}, s32[]{:T(128)}, f32[48,32]{1,0:T(8,128)}, f32[48,32,4096]{2,1,0:T(8,128)}, /*index=5*/s32[]{:T(128)}, ...), condition=%wide.region_4.5_spmd.clone, body=%wide.region_3.4_spmd.clone.sunk | while | flops 524292 | bytes 1573353 | solution.py:29
  548.4 1.2 fusion.74
  563.4 1.2 fusion.74
  572.8 1.2 fusion.74
  580.2 1.2 fusion.74
  610.3 1.3 fusion.74
  612.3 1.2 fusion.74
  617.4 2.9 multiply_reduce_fusion.1
  620.2 192.4 %all-gather.10.cloned.1.call-done = f32[48,32,4096]{2,1,0:T(8,128)} async-done(((f32[1,32,4096]{2,1,0:T(8,128)}), f32[48,32,4096]{2,1,0:T(8,128)}) %all-gather.10.cloned.1.call-update) | async-done | bytes 25165840 | tf_op jit(solution)/shard_map/all_gather | solution.py:17
  812.7 17.2 %rev.23 = f32[48,32,4096]{2,1,0:T(8,128)} reverse(f32[48,32,4096]{2,1,0:T(8,128)} %all-gather.10.cloned.1.call-done), dimensions={0} | reverse | bytes 50331648 | tf_op jit(solution)/shard_map/rev | solution.py:19
  829.9 56.9 %while.29 = (s32[]{:T(128)}, f32[32,4096]{1,0:T(8,128)S(1)}, s32[]{:T(128)}, f32[48,32]{1,0:T(8,128)S(1)}, f32[48,32,4096]{2,1,0:T(8,128)}, /*index=5*/s32[]{:T(128)}, s32[]{:T(128)}) while((s32[]{:T(128)}, f32[32,4096]{1,0:T(8,128)S(1)}, s32[]{:T(128)}, f32[48,32]{1,0:T(8,128)S(1)}, f32[48,32,4096]{2,1,0:T(8,128)}, ...), condition=%wide.region_10.11_spmd.clone, body=%wide.region_9.10_spmd.clone.sunk | while | flops 524292 | bytes 1573353 | solution.py:29
  833.5 1.2 fusion.75
  838.4 1.2 fusion.75
  842.0 1.2 fusion.75
  843.2 1.2 fusion.75
  889.3 1.4 rev.24
  890.7 1.6 fusion.12
  (289 shorter events, 159.3 us)
Async XLA Ops:
  6.5 214.3 %copy-start = (bf16[1,128,2048]{2,1,0:T(8,128)(2,1)S(1)}, bf16[1,128,2048]{2,1,0:T(8,128)(2,1)}, u32[]{:S(2)}) copy-start(bf16[1,128,2048]{2,1,0:T(8,128)(2,1)} %param.13) | copy-start | bytes 1572868
  6.5 214.3 %all-gather.6.cloned.1.call-start = ((), (), s32[]{:S(2)}) async-start(), calls=%async_computation | async-start | bytes 9609216 | tf_op jit(solution)/shard_map/all_gather | solution.py:138
  7.3 519.8 %all-gather.8.cloned.1.call-start = ((), (), s32[]{:S(2)}) async-start(), calls=%async_computation.1 | async-start | bytes 25690112 | tf_op jit(solution)/shard_map/all_gather | solution.py:17
  228.8 4.3 collective-permute-start
  236.7 3.3 copy-start.15
  236.7 5.2 copy-start.13
  236.8 5.6 copy-start.2
  237.7 575.0 %all-gather.10.cloned.1.call-start = ((), (), s32[]{:S(2)}) async-start(), calls=%async_computation.2 | async-start | bytes 25690112 | tf_op jit(solution)/shard_map/all_gather | solution.py:17
  242.6 153.3 %collective-permute-start.1 = (bf16[3,2176]{1,0:T(4,128)(2,1)S(1)}, bf16[3,2176]{1,0:T(4,128)(2,1)S(1)}, u32[]{:S(2)}, u32[]{:S(2)}) collective-permute-start(bf16[3,2176]{1,0:T(4,128)(2,1)S(1)} %copy.48), channel_id=1, source_target_pairs={{16,0},{32,16},{48,32},{64,48},{80,64},{96,80},{112,96},{128,112},... | collective-permute-start | bytes 39176 | tf_op jit(solution)/shard_map/ppermute | solution.py:40
  398.5 16.6 %copy-start.3 = (bf16[128,2176]{0,1:T(8,128)(2,1)S(1)}, bf16[128,2176]{0,1:T(8,128)(2,1)}, u32[]{:S(2)}) copy-start(bf16[128,2176]{0,1:T(8,128)(2,1)} %get-tuple-element.264) | copy-start | bytes 1671172
  429.2 1.1 copy-start.4
  615.4 0.9 copy-start.17
  616.0 1.2 copy-start.5
  616.0 1.3 copy-start.7
  616.0 1.3 copy-start.9
  616.0 1.3 copy-start.12
  886.8 1.0 copy-start.6
  886.9 1.0 copy-start.8
  886.9 1.0 copy-start.10
  886.9 1.0 copy-start.11
  886.9 1.0 copy-start.14
  886.9 1.0 copy-start.16
  890.7 2.7 copy-start.1
Sparse Core Ops, SparseCore 0:
  9.7 211.1 all-gather.5
  237.8 289.2 all-gather.7
  530.8 281.8 all-gather.9
where the time goes:
time: 908 us; the launch traced here: 900 us
  waiting for transfers between devices  496 us (55%)
  blocking collectives  148 us (16%)
  other arithmetic  131 us (14%)
  local copies, waits for them, and re-layouts  90.2 us (10%)
  between operations  14.9 us (2%)
  matrix products  12.7 us (1%)
    all_gather x2, waiting for transfers between devices, prefix(): pieces = jax.tree.map(lambda part: lax.all_gather(part, axis), value)  288 us
    all_gather x1, waiting for transfers between devices, project(): lax.all_gather(in_weight, ('fsdp', 'batch'), axis=0, tiled=True)  207 us
    all_gather x2, blocking collectives, prefix(): pieces = jax.tree.map(lambda part: lax.all_gather(part, axis), value)  148 us
    select_n x94, other arithmetic, turn(): jnp.where(position < mine, new, old)  110 us
    mul x94, local copies, waits for them, and re-layouts, chain_combine(): return (earlier[0] * later[0], later[0][:, None] * earlier[1] + later[1])  32.8 us
    slice x4, local copies, waits for them, and re-layouts, conv_silu(): padded[tap:tap + length].astype(jnp.float32)  24.3 us
  transfers between devices with their start and end apart: 5, of which 4 were waited for; matrix products, arithmetic and copies ran while one was open for 16% of the time, Pallas kernels for 0%

commit v1 on v0

v1 whole, which is shorter than its diff:
```python
import functools

import jax
import jax.numpy as jnp
from jax import lax
from jax.experimental import pallas as pl
from jax.experimental.pallas import tpu as pltpu
from jax.sharding import PartitionSpec as P

MESH = pl.DeviceIdType.MESH
HEADS = 32
HEAD_DIM = 64
STATE = 64
BLOCK = 128
INNER = 2048
HALF = 1024
COLS = 1280
HALO = 16
ROWS = 2 * BLOCK + 2 * HALO
F32 = jnp.float32
BF16 = jnp.bfloat16


def kernel(
    cfg,
    hid_ref,
    w_ref,
    marks_ref,
    cw_ref,
    cb_ref,
    dtb_ref,
    dec_ref,
    skip_ref,
    gain_ref,
    out_ref,
    wb,
    hidb,
    proj,
    xs,
    ys,
    lk,
    ls,
    fs,
    fb,
    r1,
    rf1,
    gb,
    gf,
    tb,
    tr,
    o4,
    sin,
    outb,
    par,
    cum_s,
    cumt_s,
    stept_s,
    tail_s,
    lead_s,
    msc_s,
    bt_s,
    cr_s,
    fade_s,
    w_ss,
    w_rs,
    h_ss,
    h_rs,
    l_ss,
    l_rs,
    g_ss,
    g_rs,
    o_sem,
):
    nx, ny, nz, zl, zh_n, seqs = cfg
    ql = HALF // zl
    tq = ql // 128
    s = lax.axis_index("seq")
    x = lax.axis_index("fsdp")
    y = lax.axis_index("batch")
    core = lax.rem(s, 2)
    chip = lax.div(s, 2)
    chips = seqs // 2
    z = lax.rem(chip, nz)
    yh = lax.div(chip, nz)
    q = lax.rem(z, zl)
    zh = lax.div(z, zl)

    def dev(seq, xx=x, yy=y):
        return {"seq": seq, "fsdp": xx, "batch": yy}

    def at_z(zz):
        return dev((yh * nz + zz) * 2 + core)

    partner = dev(chip * 2 + 1 - core)
    xp, xm = dev(s, lax.rem(x + 1, nx)), dev(s, lax.rem(x + nx - 1, nx))
    wrap_p = lax.div(y + 1, ny)
    wrap_m = 1 - lax.div(y + ny - 1, ny)
    yp = dev(lax.rem(s + (seqs // 2) * wrap_p, seqs), x, lax.rem(y + 1, ny))
    ym = dev(lax.rem(s + (seqs // 2) * wrap_m, seqs), x, lax.rem(y + ny - 1, ny))
    nxt = lax.rem(chip + 1, chips)
    prv = lax.rem(chip + chips - 1, chips)
    zl_peers = [at_z(zh * zl + lax.rem(q + k, zl)) for k in range(1, zl)]
    zh_peers = [at_z(lax.rem(zh + k, zh_n) * zl + q) for k in range(1, zh_n)]
    y_peer = dev(((1 - yh) * nz + z) * 2 + core)

    kb = w_ref.shape[0]
    wb[0, 0, :, 0:HALF] = w_ref[:, pl.ds(pl.multiple_of(core * HALF, HALF), HALF)]
    wb[0, 0, :, HALF : HALF + 128] = w_ref[:, INNER : INNER + 128]
    wb[0, 0, :, HALF + 128 :] = jnp.zeros((kb, 128), BF16)
    wb[0, 0, :, HALF + 128 : HALF + 160] = w_ref[:, INNER + 128 : INNER + 160]
    par[...] = jnp.zeros_like(par)
    par[0:2, 0:HEADS] = dtb_ref[...]
    par[2:4, 0:HEADS] = dec_ref[...]
    fs[...] = jnp.zeros_like(fs)
    own_rows = pl.ds(pl.multiple_of(HALO + core * BLOCK, HALO), BLOCK)
    hidb[own_rows, :] = hid_ref[0]

    barrier = pltpu.get_barrier_semaphore()
    greet = [partner, dev(nxt * 2), dev(nxt * 2 + 1), dev(prv * 2), dev(prv * 2 + 1)]
    greet += zl_peers + zh_peers + [y_peer]
    if nx > 1:
        greet += [xp, xm, yp, ym]
    for peer in greet:
        pl.semaphore_signal(barrier, inc=1, device_id=peer, device_id_type=MESH)
    pl.semaphore_wait(barrier, len(greet))

    def remote(src, dst, ssem, rsem, peer):
        return pltpu.make_async_remote_copy(
            src_ref=src,
            dst_ref=dst,
            send_sem=ssem,
            recv_sem=rsem,
            device_id=peer,
            device_id_type=MESH,
        )

    sent = []

    msgs = {}

    def w_send(half, a, b, r0, n, axis, step, tag):
        swap = half == 1
        dim_x = (axis == 1) != swap
        i, j = (b, a) if swap else (a, b)
        ii = (i + step) % nx if dim_x else i
        jj = j if dim_x else (j + step) % ny
        peer = (xp if step > 0 else xm) if dim_x else (yp if step > 0 else ym)
        k = len(msgs)
        rows = pl.ds(half * (kb // 2) + r0, n)
        copy = remote(wb.at[i, j, rows, :], wb.at[ii, jj, rows, :], w_ss.at[k], w_rs.at[k], peer)
        copy.start()
        sent.append(copy)
        aa, bb = (jj, ii) if swap else (ii, jj)
        msgs[(half, aa, bb, tag)] = copy

    def w_wait(half, a, b, tag=0):
        msgs[(half, a, b, tag)].wait_recv()

    hk = kb // 2
    halves = (0, 1)
    if nx > 1:
        for h in halves:
            w_send(h, 0, 0, 0, hk, 1, 1, 0)
            w_send(h, 0, 0, 0, hk, 1, -1, 0)

    pc = remote(hid_ref.at[0], hidb.at[own_rows, :], h_ss.at[0], h_rs.at[0], partner)
    pc.start()
    sent.append(pc)
    target = core * nxt + (1 - core) * prv
    src_rows = pl.ds(pl.multiple_of((BLOCK - HALO) * core, HALO), HALO)
    dst_rows = pl.ds(pl.multiple_of((HALO + 2 * BLOCK) * (1 - core), HALO), HALO)
    for c in range(2):
        copy = remote(
            hid_ref.at[0, src_rows, :],
            hidb.at[dst_rows, :],
            h_ss.at[1 + c],
            h_rs.at[2 - core],
            dev(target * 2 + c),
        )
        copy.start()
        sent.append(copy)

    if nx > 1:
        for h in halves:
            w_send(h, 0, 0, 0, hk, 2, 1, 0)
            w_send(h, 0, 0, 0, hk, 2, -1, 0)
        for h in halves:
            w_wait(h, 1, 0)
            w_send(h, 1, 0, 0, hk // 2, 1, 1, 0)
            w_wait(h, 3, 0)
            w_send(h, 3, 0, hk // 2, hk // 2, 1, -1, 1)
        for h in halves:
            for a in (1, 3):
                w_send(h, a, 0, 0, hk, 2, 1, 0)
                w_send(h, a, 0, 0, hk, 2, -1, 0)
        for h in halves:
            w_wait(h, 0, 1)
            w_send(h, 0, 1, 0, hk, 2, 1, 0)
        for h in halves:
            w_wait(h, 2, 0, 0)
            w_wait(h, 2, 0, 1)
            w_send(h, 2, 0, 0, hk, 2, 1, 0)
            w_send(h, 2, 0, 0, hk, 2, -1, 0)
        for h in halves:
            w_wait(h, 1, 1)
            w_send(h, 1, 1, 0, hk, 2, 1, 0)
            w_wait(h, 3, 3)
            w_send(h, 3, 3, 0, hk, 2, -1, 0)
        for h in halves:
            w_wait(h, 2, 3)
            w_send(h, 2, 3, 0, hk, 2, -1, 0)
        for h in halves:
            for a, b in ((0, 3), (1, 3), (3, 1), (2, 1), (0, 2), (1, 2), (3, 2), (2, 2)):
                w_wait(h, a, b)

    pc.wait_recv()
    for side in range(2):
        rows = pl.ds((HALO + 2 * BLOCK) * side, HALO)
        remote(
            hid_ref.at[0, 0:HALO, :], hidb.at[rows, :], h_ss.at[1], h_rs.at[1 + side], partner
        ).wait_recv()

    proj[...] = jnp.zeros_like(proj)
    if nx > 1:

        @pl.loop(0, nx * ny // 2)
        def _(t):
            i = lax.div(t, ny // 2)
            j = lax.rem(t, ny // 2) * 2
            kx = lax.rem(x + nx - i, nx) * ny
            k0 = kx + lax.rem(y + ny - j, ny)
            k1 = kx + lax.rem(y + ny - j - 1, ny)
            left = jnp.concatenate(
                [
                    hidb[:, pl.ds(pl.multiple_of(k0 * kb, kb), kb)],
                    hidb[:, pl.ds(pl.multiple_of(k1 * kb, kb), kb)],
                ],
                axis=1,
            )
            right = wb[i, pl.ds(j, 2)].reshape(2 * kb, COLS)
            proj[...] += jnp.dot(left, right, preferred_element_type=F32)

    else:
        proj[...] = jnp.dot(hidb[...], wb[0, 0], preferred_element_type=F32)
    proj[...] = proj[...].astype(BF16).astype(F32)
    first_f = jnp.where(chip == 0, 0.0, 1.0)
    last_f = jnp.where(chip == chips - 1, 0.0, 1.0)
    proj[0:HALO, :] = proj[0:HALO, :] * first_f
    proj[HALO + 2 * BLOCK :, :] = proj[HALO + 2 * BLOCK :, :] * last_f

    def conv(d, lanes, wlanes):
        total = jnp.broadcast_to(cb_ref[d : d + 1, wlanes], (2 * BLOCK, 128))
        for k in range(4):
            r0 = HALO - 3 + k if d == 0 else HALO + 3 - k
            total = total + cw_ref[d, k : k + 1, wlanes] * proj[pl.ds(r0, 2 * BLOCK), lanes]
        return total * jax.nn.sigmoid(total)

    row_i = lax.broadcasted_iota(jnp.int32, (128, 128), 0)
    lane_i = lax.broadcasted_iota(jnp.int32, (128, 128), 1)
    low = lane_i < HEAD_DIM
    low1 = lax.broadcasted_iota(jnp.int32, (1, 128), 1) < HEAD_DIM

    def seg_at(v):
        total = jnp.int32(0)
        for m in range(4):
            total = total + jnp.where(marks_ref[0, m] <= v, 1, 0)
        return total

    for d in range(2):
        bc = conv(d, slice(HALF, HALF + 128), slice(INNER, INNER + 128))
        pd = par[d : d + 1, :]
        pr = par[2 + d : 3 + d, :]
        pd = jnp.where(core == 0, pd, pltpu.roll(pd, 112, 1))
        pr = jnp.where(core == 0, pr, pltpu.roll(pr, 112, 1))
        tri = (lane_i <= row_i) if d == 0 else (lane_i >= row_i)
        trif = jnp.where(tri, 1.0, 0.0)
        for j in range(2):
            n = d * 2 + j
            t0 = chip * (2 * BLOCK) + j * BLOCK
            st = proj[HALO + j * BLOCK : HALO + (j + 1) * BLOCK, HALF + 128 :]
            st = jnp.where(core == 0, st, pltpu.roll(st, 112, 1))
            pre = st + pd
            step = jnp.maximum(pre, 0.0) + jnp.log1p(jnp.exp(-jnp.abs(pre)))
            rate = -step * pr
            cum = jnp.dot(
                trif, rate, preferred_element_type=F32, precision=lax.Precision.HIGHEST
            )
            cum_s[n] = cum
            cumt_s[n] = cum.T
            stept_s[n] = step.T
            seg_r = jnp.zeros((128, 128), jnp.int32)
            seg_c = jnp.zeros((128, 128), jnp.int32)
            for m in range(4):
                mark = marks_ref[0, m] - t0
                seg_r = seg_r + jnp.where(row_i >= mark, 1, 0)
                seg_c = seg_c + jnp.where(lane_i >= mark, 1, 0)
            in_seg, out_seg = (
                (seg_at(t0 - 1), seg_at(t0 + BLOCK - 1))
                if d == 0
                else (seg_at(t0 + BLOCK), seg_at(t0))
            )
            base = seg_at(t0 - 1) * 0
            last = cum[BLOCK - 1 : BLOCK, :] if d == 0 else cum[0:1, :]
            lead_s[n] = jnp.where(seg_r == in_seg - base, jnp.exp(cum), 0.0)
            tail_s[n] = jnp.where(seg_r == out_seg, jnp.exp(last - cum), 0.0) * step
            same = jnp.where(in_seg == out_seg, 1.0, 0.0)
            fade_s[n : n + 1, :] = jnp.exp(last) * same
            bcj = bc[j * BLOCK : (j + 1) * BLOCK, :]
            b_only = jnp.where(low, bcj, 0.0).astype(BF16)
            c_low = pltpu.roll(bcj, HEAD_DIM, 1).astype(BF16)
            scores = lax.dot_general(
                c_low, b_only, (((1,), (1,)), ((), ())), preferred_element_type=F32
            )
            msc_s[n] = jnp.where(tri & (seg_r == seg_c), scores, 0.0)
            bt_s[n] = bcj.T[0:STATE, :].astype(BF16)
            cr_s[n] = c_low

    def pair(value, mask):
        return jnp.where(mask, value[:, 0:1], value[:, 1:2])

    def lanes_of(p):
        return pl.ds(pl.multiple_of(p * 128, 128), 128)

    order = ((0, 1), (1, 0))

    @pl.loop(0, HALF // 128)
    def _(p):
        lanes = lanes_of(p)
        wl = pl.ds(pl.multiple_of(core * HALF + p * 128, 128), 128)
        quarter = lax.div(p, tq)
        inner = pl.ds(pl.multiple_of(lax.rem(p, tq) * 128, 128), 128)
        shift = 128 - 2 * p
        fades = pltpu.roll(fade_s[...], shift, 1)
        for d in range(2):
            xc = conv(d, lanes, wl).astype(BF16)
            xs[d, :, lanes] = xc
            ends = []
            for j in range(2):
                tails = pair(pltpu.roll(tail_s[d * 2 + j], shift, 1), low)
                inp = (tails * xc[j * BLOCK : (j + 1) * BLOCK, :].astype(F32)).astype(BF16)
                ends.append(jnp.dot(bt_s[d * 2 + j], inp, preferred_element_type=F32))
            f, g = order[d]
            fade_f = pair(fades[d * 2 + f : d * 2 + f + 1, :], low1)
            fade_g = pair(fades[d * 2 + g : d * 2 + g + 1, :], low1)
            lk[d, :, lanes] = ends[f]
            fb[d : d + 1, lanes] = fade_f
            ls[quarter, d, :, inner] = (fade_g * ends[f] + ends[g]).astype(BF16)
            fs[quarter, d : d + 1, inner] = fade_f * fade_g

    def local_pairs(lo, hi):
        @pl.loop(lo, hi)
        def _(p):
            lanes = lanes_of(p)
            shift = 128 - 2 * p
            head = core * (HEADS // 2) + 2 * p
            for d in range(2):
                skips = jnp.where(low1, skip_ref[d, head], skip_ref[d, head + 1])
                for j in range(2):
                    n = d * 2 + j
                    rows = slice(j * BLOCK, (j + 1) * BLOCK)
                    xt = xs[d, rows, lanes]
                    cums = pltpu.roll(cum_s[n], shift, 1)
                    ws = []
                    for hh in range(2):
                        h = pl.ds(2 * p + hh, 1)
                        gap = jnp.minimum(cums[:, hh : hh + 1] - cumt_s[n, h, :], 0.0)
                        ws.append((jnp.exp(gap) * msc_s[n] * stept_s[n, h, :]).astype(BF16))
                    xf = xt.astype(F32)
                    xl = jnp.where(low, xf, 0.0).astype(BF16)
                    xh = jnp.where(low, 0.0, xf).astype(BF16)
                    inner = jnp.dot(
                        jnp.concatenate(ws, axis=1),
                        jnp.concatenate([xl, xh], axis=0),
                        preferred_element_type=F32,
                    )
                    ys[d, rows, lanes] = inner + skips * xf

    copies1 = []
    for k in range(1, zl):
        to = lax.rem(q + k, zl)
        for a, (src, dst) in enumerate(((ls, r1), (fs, rf1))):
            c = remote(
                src.at[to], dst.at[q], l_ss.at[k, a], l_rs.at[k, a], zl_peers[k - 1]
            )
            c.start()
            sent.append(c)
            copies1.append(c)
    r1[q] = ls[q]
    rf1[q] = fs[q]
    local_pairs(0, 4)
    for c in copies1:
        c.wait_recv()

    groups = []
    for d in range(2):
        total = jnp.zeros((STATE, ql), F32)
        fade = jnp.ones((1, ql), F32)
        for step in range(zl):
            c = step if d == 0 else zl - 1 - step
            f = rf1[c, d : d + 1, :]
            total = f * total + r1[c, d].astype(F32)
            fade = fade * f
        gb[zh, d] = total.astype(BF16)
        groups.append(fade)
    gf[zh] = jnp.concatenate(groups + [jnp.zeros((6, ql), F32)], axis=0)
    copies2 = []
    for k in range(1, zh_n):
        for a, buf in enumerate((gb, gf)):
            c = remote(
                buf.at[zh], buf.at[zh], g_ss.at[k, a], g_rs.at[k, a], zh_peers[k - 1]
            )
            c.start()
            sent.append(c)
            copies2.append(c)
    local_pairs(4, 6)
    for c in copies2:
        c.wait_recv()

    for d in range(2):
        total = jnp.zeros((STATE, ql), F32)
        for step in range(zh_n):
            c = step if d == 0 else zh_n - 1 - step
            total = gf[c, d : d + 1, :] * total + gb[c, d].astype(F32)
        tb[d] = total.astype(BF16)
    c3 = remote(tb.at[yh], tr, g_ss.at[0, 0], g_rs.at[0, 0], y_peer)
    c3.start()
    sent.append(c3)
    local_pairs(6, 8)
    c3.wait_recv()

    for d in range(2):
        other = jnp.where(yh == (1 if d == 0 else 0), 1.0, 0.0)
        state = tr[...].astype(F32) * other
        for step in range(zh_n - 1):
            c = step if d == 0 else zh_n - 1 - step
            before = (zh > c) if d == 0 else (zh < c)
            longer = gf[c, d : d + 1, :] * state + gb[c, d].astype(F32)
            state = jnp.where(before, longer, state)
        for step in range(zl):
            c = step if d == 0 else zl - 1 - step
            o4[c, d] = state.astype(BF16)
            if step < zl - 1:
                state = rf1[c, d : d + 1, :] * state + r1[c, d].astype(F32)

    copies4 = []
    for k in range(1, zl):
        to = lax.rem(q + k, zl)
        c = remote(o4.at[to], sin.at[q], l_ss.at[0, k], l_rs.at[0, k], zl_peers[k - 1])
        c.start()
        sent.append(c)
        copies4.append(c)
    sin[q] = o4[q]

    ones = jnp.where((row_i < HEAD_DIM) == low, 1.0 / HEAD_DIM, 0.0).astype(BF16)

    def finish(quarter):
        @pl.loop(0, tq)
        def _(t):
            p = quarter * tq + t
            lanes = lanes_of(p)
            inner = lanes_of(t)
            shift = 128 - 2 * p
            wl = pl.ds(pl.multiple_of(core * HALF + p * 128, 128), 128)
            mixed = [None, None]
            for d in range(2):
                gains = gain_ref[d : d + 1, wl]
                entering = sin[quarter, d, :, inner]
                second = fb[d : d + 1, lanes] * entering.astype(F32) + lk[d, :, lanes]
                f, g = order[d]
                states = {f: entering, g: second.astype(BF16)}
                for j in range(2):
                    n = d * 2 + j
                    rows = slice(j * BLOCK, (j + 1) * BLOCK)
                    carried = jnp.dot(
                        cr_s[n, :, 0:STATE], states[j], preferred_element_type=F32
                    )
                    leads = pair(pltpu.roll(lead_s[n], shift, 1), low)
                    yv = ys[d, rows, lanes] + leads * carried
                    sq = yv * yv
                    hi = sq.astype(BF16)
                    lo = (sq - hi.astype(F32)).astype(BF16)
                    mean = jnp.dot(hi, ones, preferred_element_type=F32) + jnp.dot(
                        lo, ones, preferred_element_type=F32
                    )
                    res = yv * lax.rsqrt(mean + 1e-05) * gains
                    mixed[j] = res if d == 0 else mixed[j] + res
            for j in range(2):
                outb[j, :, lanes] = mixed[j].astype(BF16)

    finish(q)
    for k in range(1, zl):
        copies4[k - 1].wait_recv()
        finish(lax.rem(q + zl - k, zl))

    cols = pl.ds(pl.multiple_of(core * HALF, HALF), HALF)
    oc = remote(outb.at[1 - core], out_ref.at[0, :, cols], o_sem.at[0], o_sem.at[1], partner)
    oc.start()
    own = pltpu.make_async_copy(outb.at[core], out_ref.at[0, :, cols], o_sem.at[2])
    own.start()
    own.wait()
    oc.wait()
    for c in sent:
        c.wait_send()


def solution(mesh):
    nx, ny, seqs = mesh.shape["fsdp"], mesh.shape["batch"], mesh.shape["seq"]
    nz = seqs // 4
    zl = 4 if nz % 4 == 0 and nz > 4 else 2
    zh_n = nz // zl
    ql = HALF // zl
    cfg = (nx, ny, nz, zl, zh_n, seqs)

    def on_device(hidden, in_weight, marks, cw, cb, dtb, dec, skip, gain):
        kb = in_weight.shape[0]
        vmem = pl.BlockSpec(memory_space=pltpu.VMEM)
        smem = pl.BlockSpec(memory_space=pltpu.SMEM)
        dma = pltpu.SemaphoreType.DMA
        return pl.pallas_call(
            functools.partial(kernel, cfg),
            out_shape=jax.ShapeDtypeStruct(hidden.shape, BF16),
            in_specs=[vmem, vmem, smem, vmem, vmem, vmem, vmem, smem, vmem],
            out_specs=pl.BlockSpec(memory_space=pl.ANY),
            scratch_shapes=[
                pltpu.VMEM((nx, ny, kb, COLS), BF16),
                pltpu.VMEM((ROWS, INNER), BF16),
                pltpu.VMEM((ROWS, COLS), F32),
                pltpu.VMEM((2, 2 * BLOCK, HALF), BF16),
                pltpu.VMEM((2, 2 * BLOCK, HALF), F32),
                pltpu.VMEM((2, STATE, HALF), F32),
                pltpu.VMEM((zl, 2, STATE, ql), BF16),
                pltpu.VMEM((zl, 8, ql), F32),
                pltpu.VMEM((8, HALF), F32),
                pltpu.VMEM((zl, 2, STATE, ql), BF16),
                pltpu.VMEM((zl, 8, ql), F32),
                pltpu.VMEM((zh_n, 2, STATE, ql), BF16),
                pltpu.VMEM((zh_n, 8, ql), F32),
                pltpu.VMEM((2, STATE, ql), BF16),
                pltpu.VMEM((STATE, ql), BF16),
                pltpu.VMEM((zl, 2, STATE, ql), BF16),
                pltpu.VMEM((zl, 2, STATE, ql), BF16),
                pltpu.VMEM((2, BLOCK, HALF), BF16),
                pltpu.VMEM((8, 128), F32),
                pltpu.VMEM((4, 128, 128), F32),
                pltpu.VMEM((4, 128, 128), F32),
                pltpu.VMEM((4, 128, 128), F32),
                pltpu.VMEM((4, 128, 128), F32),
                pltpu.VMEM((4, 128, 128), F32),
                pltpu.VMEM((4, 128, 128), F32),
                pltpu.VMEM((4, STATE, 128), BF16),
                pltpu.VMEM((4, 128, 128), BF16),
                pltpu.VMEM((8, 128), F32),
                dma((40,)),
                dma((40,)),
                dma((3,)),
                dma((3,)),
                dma((4, 4)),
                dma((4, 4)),
                dma((3, 2)),
                dma((3, 2)),
                dma((3,)),
            ],
            compiler_params=pltpu.CompilerParams(
                collective_id=0, has_side_effects=True, vmem_limit_bytes=48 * 1024 * 1024
            ),
        )(hidden, in_weight, marks, cw, cb, dtb, dec, skip, gain)

    group = P(("fsdp", "batch"), "seq", None)
    rows = P(("fsdp", "batch"), None)
    return jax.shard_map(
        on_device,
        mesh=mesh,
        in_specs=(group, rows, rows, P(), P(), P(), P(), P(), P()),
        out_specs=group,
        check_vma=False,
    )
```

time: 908 us -> 91.4 us (0.10)
  waiting for transfers between devices: 496 us -> 0 us
  blocking collectives: 148 us -> 0 us
  other arithmetic: 131 us -> 0 us
  Pallas kernels: 0 us -> 88.9 us
  local copies, waits for them, and re-layouts: 90.2 us -> 2.2 us
  between operations: 14.9 us -> 0.12 us
  matrix products: 12.7 us -> 0 us
    all_gather x3 -> x0, waiting for transfers between devices: 495 us -> none  [the longest x2 288 us: prefix(): pieces = jax.tree.map(lambda part: lax.all_gather(part, axis), value)]
    all_gather x2 -> x0, blocking collectives: 148 us -> none  [prefix(): pieces = jax.tree.map(lambda part: lax.all_gather(part, axis), value)]
    select_n x95 -> x0, other arithmetic: 111 us -> none  [the longest x94 110 us: turn(): jnp.where(position < mine, new, old)]
    pallas_call x0 -> x1, Pallas kernels: none -> 88.9 us  [on_device(): pl.pallas_call(functools.partial(kernel, cfg), out_shape=jax.ShapeDtypeSt...]
    mul x96 -> x0, local copies, waits for them, and re-layouts: 34.1 us -> none  [the longest x94 32.8 us: chain_combine(): return (earlier[0] * later[0], later[0][:, None] * earlier[1] + later[1])]
    slice x14 -> x0, local copies, waits for them, and re-layouts: 29.1 us -> none  [the longest x4 24.3 us: conv_silu(): padded[tap:tap + length].astype(jnp.float32)]
    rev x5 -> x0, local copies, waits for them, and re-layouts: 18.8 us -> none  [the longest x2 17.2 us: prefix(): pieces = jax.tree.map(lambda part: part[::-1], pieces)]
    dot_general x9 -> x0, matrix products: 12.7 us -> none  [the longest x1 6.09 us: project(): jnp.dot(rows_in, lax.all_gather(in_weight, ('fsdp', 'batch'), axis=0, til...]
  transfers between devices with their start and end apart: 5 -> 0, of which waited for: 4 -> 0; matrix products, arithmetic and copies ran while one was open for 16% -> 0% of each run, Pallas kernels for 0% -> 0%
where the time goes in v1:
time: 91.4 us; the launch traced here: 91.3 us
  Pallas kernels  88.9 us (97%)
  local copies, waits for them, and re-layouts  2.2 us (2%)
    pallas_call x1, Pallas kernels, on_device(): pl.pallas_call(functools.partial(kernel, cfg), out_shape=jax.ShapeDtypeSt...  88.9 us
    unnamed x18, local copies, waits for them, and re-layouts  2.2 us

profile of v1, /device:TPU:1, one launch (start us, length us, event | category | flops | bytes accessed | tf_op | source)
XLA Modules:
  0.0 91.3 jit_solution(6940790307672444126)
XLA Ops:
  0.0 0.0 copy-start.3
  0.0 0.0 copy-start.6
  0.0 0.0 copy-start.5
  0.0 0.0 copy-start.4
  0.0 0.0 copy-start.2
  0.0 0.0 copy-start.1
  0.0 0.0 copy-start.7
  0.0 0.0 copy-start
  0.1 1.4 %copy.10.w_ref = bf16[128,2208]{1,0:T(8,128)(2,1)S(1)} copy(bf16[128,2208]{0,1:T(8,128)(2,1)} %param.10) | data formatting | bytes 1130496 | tf_op args[1]
  1.4 0.0 copy-done.3
  1.4 0.0 copy-done.6
  1.5 0.0 copy-done.5
  1.5 0.0 copy-done.4
  1.5 0.0 copy-done.2
  1.5 0.0 copy-done.1
  1.5 0.0 copy-done.7
  1.5 0.0 copy-done
  1.5 88.9 %shard_map.91 = bf16[1,128,2048]{2,1,0:T(8,128)(2,1)S(1)} custom-call(bf16[1,128,2048]{2,1,0:T(8,128)(2,1)S(1)} %copy-done, bf16[128,2208]{1,0:T(8,128)(2,1)S(1)} %copy.10.w_ref, s32[1,4]{1,0:T(1,128)S(1)} %copy-done.7, f32[2,4,2176]{2,1,0:T(4,128)S(1)} %copy-done.1, f32[2,2176]{1,0:T(2,128)S(1)} %copy-done.2, f32[2,32]{1,0:T(2,128)S(1)} %copy-done.4, ...), custom_call_target="tpu_custom_call" | custom-call | tf_op jit(solution)/shard_map/pallas_call | solution.py:519
  90.5 0.8 copy.12
Async XLA Ops:
  0.0 1.4 %copy-start.3 = (f32[2,2048]{1,0:T(2,128)S(1)}, f32[2,2048]{1,0:T(2,128)}, u32[]{:S(2)}) copy-start(f32[2,2048]{1,0:T(2,128)} %gain_ref.1) | copy-start | bytes 49156
  0.0 1.4 %copy-start.6 = (f32[2,32]{1,0:T(2,128)S(1)}, f32[2,32]{1,0:T(2,128)}, u32[]{:S(2)}) copy-start(f32[2,32]{1,0:T(2,128)} %skip_ref.1) | copy-start | bytes 772
  0.0 1.5 %copy-start.5 = (f32[2,32]{1,0:T(2,128)S(1)}, f32[2,32]{1,0:T(2,128)}, u32[]{:S(2)}) copy-start(f32[2,32]{1,0:T(2,128)} %dec_ref.1) | copy-start | bytes 772
  0.0 1.5 %copy-start.4 = (f32[2,32]{1,0:T(2,128)S(1)}, f32[2,32]{1,0:T(2,128)}, u32[]{:S(2)}) copy-start(f32[2,32]{1,0:T(2,128)} %dtb_ref.1) | copy-start | bytes 772
  0.0 1.5 %copy-start.2 = (f32[2,2176]{1,0:T(2,128)S(1)}, f32[2,2176]{1,0:T(2,128)}, u32[]{:S(2)}) copy-start(f32[2,2176]{1,0:T(2,128)} %cb_ref.1) | copy-start | bytes 52228
  0.0 1.5 %copy-start.1 = (f32[2,4,2176]{2,1,0:T(4,128)S(1)}, f32[2,4,2176]{2,1,0:T(4,128)}, u32[]{:S(2)}) copy-start(f32[2,4,2176]{2,1,0:T(4,128)} %cw_ref.1) | copy-start | bytes 208900
  0.0 1.5 %copy-start.7 = (s32[1,4]{1,0:T(1,128)S(1)}, s32[1,4]{1,0:T(1,128)}, u32[]{:S(2)}) copy-start(s32[1,4]{1,0:T(1,128)} %marks_ref.1) | copy-start | bytes 52
  0.0 1.5 %copy-start = (bf16[1,128,2048]{2,1,0:T(8,128)(2,1)S(1)}, bf16[1,128,2048]{2,1,0:T(8,128)(2,1)}, u32[]{:S(2)}) copy-start(bf16[1,128,2048]{2,1,0:T(8,128)(2,1)} %hid_ref.1) | copy-start | bytes 1572868

commit v2 on v1

v2 whole, which is shorter than its diff:
```python
import functools

import jax
import jax.numpy as jnp
from jax import lax
from jax.experimental import pallas as pl
from jax.experimental.pallas import tpu as pltpu
from jax.sharding import PartitionSpec as P

MESH = pl.DeviceIdType.MESH
HEADS = 32
HEAD_DIM = 64
STATE = 64
BLOCK = 128
INNER = 2048
HALF = 1024
PART = 384
HALO = 16
ROWS = 2 * BLOCK + 2 * HALO
F32 = jnp.float32
BF16 = jnp.bfloat16


def kernel(
    cfg,
    hid_ref,
    w_ref,
    marks_ref,
    cw_ref,
    cb_ref,
    dtb_ref,
    dec_ref,
    skip_ref,
    gain_ref,
    out_ref,
    wb,
    hidb,
    proj,
    tile,
    other,
    xs,
    ys,
    lk,
    ls,
    fs,
    fb,
    r1,
    rf1,
    gb,
    gf,
    tb,
    tr,
    o4,
    sin,
    outb,
    par,
    cum_s,
    cumt_s,
    stept_s,
    tail_s,
    lead_s,
    msc_s,
    bt_s,
    cr_s,
    fade_s,
    w_ss,
    w_rs,
    h_ss,
    h_rs,
    l_ss,
    l_rs,
    g_ss,
    g_rs,
    in_sem,
    o_ss,
    o_rs,
    own_sem,
):
    nx, ny, nz, zl, zh_n, seqs = cfg
    ql = HALF // zl
    tq = ql // 128
    s = lax.axis_index("seq")
    x = lax.axis_index("fsdp")
    y = lax.axis_index("batch")
    core = lax.rem(s, 2)
    chip = lax.div(s, 2)
    chips = seqs // 2
    z = lax.rem(chip, nz)
    yh = lax.div(chip, nz)
    q = lax.rem(z, zl)
    zh = lax.div(z, zl)

    def dev(seq, xx=x, yy=y):
        return {"seq": seq, "fsdp": xx, "batch": yy}

    def at_z(zz):
        return dev((yh * nz + zz) * 2 + core)

    partner = dev(chip * 2 + 1 - core)
    xp, xm = dev(s, lax.rem(x + 1, nx)), dev(s, lax.rem(x + nx - 1, nx))
    wrap_p = lax.div(y + 1, ny)
    wrap_m = 1 - lax.div(y + ny - 1, ny)
    yp = dev(lax.rem(s + (seqs // 2) * wrap_p, seqs), x, lax.rem(y + 1, ny))
    ym = dev(lax.rem(s + (seqs // 2) * wrap_m, seqs), x, lax.rem(y + ny - 1, ny))
    nxt = lax.rem(chip + 1, chips)
    prv = lax.rem(chip + chips - 1, chips)
    rot = lax.rem(z, 3) if nx > 1 else jnp.int32(0)
    zp, zm = at_z(lax.rem(z + 1, nz)), at_z(lax.rem(z + nz - 1, nz))
    zl_peers = [at_z(zh * zl + lax.rem(q + k, zl)) for k in range(1, zl)]
    zh_peers = [at_z(lax.rem(zh + k, zh_n) * zl + q) for k in range(1, zh_n)]
    y_peer = dev(((1 - yh) * nz + z) * 2 + core)

    barrier = pltpu.get_barrier_semaphore()
    greet = [partner, dev(nxt * 2), dev(nxt * 2 + 1), dev(prv * 2), dev(prv * 2 + 1)]
    greet += zl_peers + zh_peers + [y_peer]
    if nx > 1:
        greet += [xp, xm, yp, ym, zp, zm]
    for peer in greet:
        pl.semaphore_signal(barrier, inc=1, device_id=peer, device_id_type=MESH)

    own_rows = pl.ds(pl.multiple_of(HALO + core * BLOCK, HALO), BLOCK)
    kb = w_ref.shape[1]
    reads = [(hid_ref.at[0], hidb.at[own_rows, :])]
    part_lanes = [
        pl.ds(pl.multiple_of(lax.rem(rot + u, 3) * PART, PART), PART) for u in (1, 2, 0)
    ]
    bases = [lax.rem(p + 5 - rot, 3) * PART for p in range(3)]
    cols0 = core * HALF
    for src, dst, count in (
        (cols0, bases[0], PART),
        (cols0 + PART, bases[1], PART),
        (cols0 + 2 * PART, bases[2], 256),
        (INNER + 128 * core, bases[2] + 256, 32),
        (INNER + 32, bases[2] + 288, 96),
    ):
        reads.append(
            (
                w_ref.at[pl.ds(pl.multiple_of(src, 32), count), :],
                wb.at[0, 0, pl.ds(pl.multiple_of(dst, 32), count), :],
            )
        )
    reads = [pltpu.make_async_copy(a, b, in_sem.at[k]) for k, (a, b) in enumerate(reads)]
    for c in reads:
        c.start()
    par[...] = jnp.zeros_like(par)
    par[0:2, 0:HEADS] = dtb_ref[...]
    par[2:4, 0:HEADS] = dec_ref[...]
    fade_s[...] = jnp.zeros_like(fade_s)
    for c in reads:
        c.wait()
    pl.semaphore_wait(barrier, len(greet))

    def remote(src, dst, ssem, rsem, peer):
        return pltpu.make_async_remote_copy(
            src_ref=src,
            dst_ref=dst,
            send_sem=ssem,
            recv_sem=rsem,
            device_id=peer,
            device_id_type=MESH,
        )

    sent = []

    msgs = {}
    zmsgs = {}

    def w_send(half, a, b, r0, n, axis, step, tag):
        swap = half == 1
        dim_x = (axis == 1) != swap
        i, j = (b, a) if swap else (a, b)
        ii = (i + step) % nx if dim_x else i
        jj = j if dim_x else (j + step) % ny
        peer = (xp if step > 0 else xm) if dim_x else (yp if step > 0 else ym)
        k = len(msgs)
        rows = pl.ds(half * PART + r0, n)
        copy = remote(
            wb.at[i, j, rows, :], wb.at[ii, jj, rows, :], w_ss.at[k], w_rs.at[k], peer
        )
        copy.start()
        sent.append(copy)
        aa, bb = (jj, ii) if swap else (ii, jj)
        msgs[(half, aa, bb, tag)] = copy

    def w_wait(half, a, b):
        for tag in range(2):
            if (half, a, b, tag) in msgs:
                msgs[(half, a, b, tag)].wait_recv()
        i, j = (b, a) if half == 1 else (a, b)
        k = 32 + len(zmsgs)
        copy = remote(
            wb.at[i, j, pl.ds(half * (PART + hk // 2), hk // 2), :],
            wb.at[i, j, pl.ds(2 * PART + half * (hk // 2), hk // 2), :],
            w_ss.at[k],
            w_rs.at[k],
            zm if half else zp,
        )
        copy.start()
        sent.append(copy)
        zmsgs[(half, i, j)] = copy

    hk = PART
    halves = (0, 1)
    if nx > 1:
        for h in halves:
            w_send(h, 0, 0, 0, hk, 1, 1, 0)
            w_send(h, 0, 0, 0, hk, 1, -1, 0)

    pc = remote(hid_ref.at[0], hidb.at[own_rows, :], h_ss.at[0], h_rs.at[0], partner)
    pc.start()
    sent.append(pc)
    target = core * nxt + (1 - core) * prv
    src_rows = pl.ds(pl.multiple_of((BLOCK - HALO) * core, HALO), HALO)
    dst_rows = pl.ds(pl.multiple_of((HALO + 2 * BLOCK) * (1 - core), HALO), HALO)
    for c in range(2):
        copy = remote(
            hid_ref.at[0, src_rows, :],
            hidb.at[dst_rows, :],
            h_ss.at[1 + c],
            h_rs.at[2 - core],
            dev(target * 2 + c),
        )
        copy.start()
        sent.append(copy)

    def rows_wait():
        pc.wait_recv()
        for side in range(2):
            rows = pl.ds((HALO + 2 * BLOCK) * side, HALO)
            remote(
                hid_ref.at[0, 0:HALO, :], hidb.at[rows, :], h_ss.at[1], h_rs.at[1 + side], partner
            ).wait_recv()

    def project(slots, parts, first=False):
        left = []
        for i, j in slots:
            k = lax.rem(x + nx - i, nx) * ny + lax.rem(y + ny - j, ny)
            left.append(hidb[:, pl.ds(pl.multiple_of(k * kb, kb), kb)])
        left = jnp.concatenate(left, axis=1)
        for u in parts:
            rows = slice(u * PART, (u + 1) * PART)
            right = jnp.concatenate([wb[i, j, rows, :] for i, j in slots], axis=1)
            value = lax.dot_general(
                left, right, (((1,), (1,)), ((), ())), preferred_element_type=F32
            )
            if first:
                proj[:, part_lanes[u]] = value
            else:
                proj[:, part_lanes[u]] += value

    if nx > 1:
        xy, zz = (0, 1), (2,)
        order_k = (
            ((0, 0), (0, 1)),
            ((1, 0), (0, 3)),
            ((3, 0), (1, 1)),
            ((3, 3), (1, 3)),
            ((3, 1), (0, 2)),
            ((2, 0), (2, 1)),
            ((1, 2), (3, 2)),
            ((2, 3), (2, 2)),
        )
        for h in halves:
            w_send(h, 0, 0, 0, hk, 2, 1, 0)
            w_send(h, 0, 0, 0, hk, 2, -1, 0)
        for h in halves:
            w_wait(h, 1, 0)
            w_send(h, 1, 0, 0, hk // 2, 1, 1, 0)
            w_wait(h, 3, 0)
            w_send(h, 3, 0, hk // 2, hk // 2, 1, -1, 1)
        for h in halves:
            for a in (1, 3):
                w_send(h, a, 0, 0, hk, 2, 1, 0)
                w_send(h, a, 0, 0, hk, 2, -1, 0)
        rows_wait()
        for h in halves:
            w_wait(h, 0, 1)
            w_send(h, 0, 1, 0, hk, 2, 1, 0)
            w_wait(h, 0, 3)
        project(order_k[0], xy, True)
        for h in halves:
            w_wait(h, 2, 0)
            w_send(h, 2, 0, 0, hk, 2, 1, 0)
            w_send(h, 2, 0, 0, hk, 2, -1, 0)
        project(order_k[1], xy)
        for h in halves:
            w_wait(h, 1, 1)
            w_send(h, 1, 1, 0, hk, 2, 1, 0)
            w_wait(h, 3, 3)
            w_send(h, 3, 3, 0, hk, 2, -1, 0)
        project(order_k[2], xy)
        for h in halves:
            w_wait(h, 1, 3)
            w_wait(h, 3, 1)
        project(order_k[3], xy)
        for h in halves:
            w_wait(h, 2, 3)
            w_send(h, 2, 3, 0, hk, 2, -1, 0)
            w_wait(h, 0, 2)
        project(order_k[4], xy)
        for h in halves:
            w_wait(h, 2, 1)
            w_wait(h, 1, 2)
        project(order_k[5], xy)

        def z_wait(slots):
            for i, j in slots:
                for h in halves:
                    if (i, j) != (0, 0):
                        zmsgs[(h, i, j)].wait_recv()

        z_wait(order_k[0])
        project(order_k[0], zz, True)
        z_wait(order_k[1])
        project(order_k[1], zz)
        for h in halves:
            w_wait(h, 3, 2)
        project(order_k[6], xy)
        for h in halves:
            w_wait(h, 2, 2)
        project(order_k[7], xy)
        for slots in order_k[2:]:
            z_wait(slots)
            project(slots, zz)
    else:
        rows_wait()
        project(((0, 0),), (0, 1, 2), True)

    tile[...] = proj[:, HALF : HALF + 128].astype(BF16)
    swap_tile = remote(tile, other, h_ss.at[3], h_rs.at[3], partner)
    swap_tile.start()
    sent.append(swap_tile)
    first_f = jnp.where(chip == 0, 0.0, 1.0)
    last_f = jnp.where(chip == chips - 1, 0.0, 1.0)

    def ends_off(lanes):
        proj[0:HALO, lanes] = proj[0:HALO, lanes] * first_f
        proj[HALO + 2 * BLOCK :, lanes] = proj[HALO + 2 * BLOCK :, lanes] * last_f

    proj[:, 0:HALF] = proj[:, 0:HALF].astype(BF16).astype(F32)
    ends_off(slice(0, HALF))

    def conv(d, lanes, wlanes):
        total = jnp.broadcast_to(cb_ref[d : d + 1, wlanes], (2 * BLOCK, 128))
        for k in range(4):
            r0 = HALO - 3 + k if d == 0 else HALO + 3 - k
            total = total + cw_ref[d, k : k + 1, wlanes] * proj[pl.ds(r0, 2 * BLOCK), lanes]
        return total * jax.nn.sigmoid(total)

    row_i = lax.broadcasted_iota(jnp.int32, (128, 128), 0)
    lane_i = lax.broadcasted_iota(jnp.int32, (128, 128), 1)
    low = lane_i < HEAD_DIM
    low8 = lax.broadcasted_iota(jnp.int32, (8, 128), 1) < HEAD_DIM
    low1 = lax.broadcasted_iota(jnp.int32, (1, 128), 1) < HEAD_DIM

    def seg_at(v):
        total = jnp.int32(0)
        for m in range(4):
            total = total + jnp.where(marks_ref[0, m] <= v, 1, 0)
        return total

    def pair(value, mask):
        return jnp.where(mask, value[:, 0:1], value[:, 1:2])

    def lanes_of(p):
        return pl.ds(pl.multiple_of(p * 128, 128), 128)

    @pl.loop(0, HALF // 128)
    def _(p):
        wl = pl.ds(pl.multiple_of(core * HALF + p * 128, 128), 128)
        for d in range(2):
            xs[d, :, lanes_of(p)] = conv(d, lanes_of(p), wl).astype(BF16)

    def summary(d, quarter):
        fades_d = [fade_s[d * 2 + d], fade_s[d + 1]]
        for t in range(tq):
            p = quarter * tq + t
            lanes = lanes_of(p)
            inner = slice(t * 128, (t + 1) * 128)
            shift = 128 - 2 * p
            ends, fades = [], []
            for o, j in enumerate((d, 1 - d)):
                n = d * 2 + j
                rows = pl.ds(pl.multiple_of(j * BLOCK, BLOCK), BLOCK)
                tails = pair(pltpu.roll(tail_s[n], shift, 1), low)
                inp = (tails * xs[d, rows, lanes].astype(F32)).astype(BF16)
                ends.append(jnp.dot(bt_s[n], inp, preferred_element_type=F32))
                fades.append(pair(pltpu.roll(fades_d[o], shift, 1), low8)[0:1, :])
            lk[d, :, lanes] = ends[0]
            fb[d, 0:1, lanes] = fades[0]
            ls[d, quarter, :, inner] = (fades[1] * ends[0] + ends[1]).astype(BF16)
            fs[d, quarter, :, inner] = fades[0] * fades[1]

    def level1(ph, d):
        copies = []
        for k in sorted(range(zl), key=lambda k: (k == 0, abs(k - zl // 2))):
            to = lax.rem(q + k, zl)
            summary(d, to)
            if k == 0:
                r1[d, q] = ls[d, q]
                rf1[d, q] = fs[d, q]
                continue
            for a, (src, dst) in enumerate(((ls, r1), (fs, rf1))):
                c = remote(
                    src.at[d, to],
                    dst.at[d, q],
                    l_ss.at[ph, k, a],
                    l_rs.at[ph, k, a],
                    zl_peers[k - 1],
                )
                c.start()
                sent.append(c)
                copies.append(c)
        return copies

    d_a, d_b = yh, 1 - yh
    swap_tile.wait_recv()
    mine, theirs = tile[...].astype(F32), other[...].astype(F32)
    proj[:, HALF : HALF + 128] = jnp.where(core == 0, mine, theirs)
    proj[:, HALF + 128 :] = jnp.where(core == 0, theirs, mine)
    ends_off(slice(HALF, HALF + 128))

    for d in range(2):
        bc = conv(d, slice(HALF, HALF + 128), slice(INNER, INNER + 128))
        pd = par[d : d + 1, :]
        pr = par[2 + d : 3 + d, :]
        pd = jnp.where(core == 0, pd, pltpu.roll(pd, 112, 1))
        pr = jnp.where(core == 0, pr, pltpu.roll(pr, 112, 1))
        tri = (lane_i <= row_i) if d == 0 else (lane_i >= row_i)
        trif = jnp.where(tri, 1.0, 0.0)
        for j in range(2):
            n = d * 2 + j
            t0 = chip * (2 * BLOCK) + j * BLOCK
            st = proj[HALO + j * BLOCK : HALO + (j + 1) * BLOCK, HALF + 128 :]
            st = jnp.where(core == 0, st, pltpu.roll(st, 112, 1))
            pre = st + pd
            step = jnp.maximum(pre, 0.0) + jnp.log1p(jnp.exp(-jnp.abs(pre)))
            rate = -step * pr
            cum = jnp.dot(
                trif, rate, preferred_element_type=F32, precision=lax.Precision.HIGHEST
            )
            cum_s[n] = cum
            cumt_s[n] = cum.T
            stept_s[n] = step.T
            seg_r = jnp.zeros((128, 128), jnp.int32)
            seg_c = jnp.zeros((128, 128), jnp.int32)
            for m in range(4):
                mark = marks_ref[0, m] - t0
                seg_r = seg_r + jnp.where(row_i >= mark, 1, 0)
                seg_c = seg_c + jnp.where(lane_i >= mark, 1, 0)
            in_seg, out_seg = (
                (seg_at(t0 - 1), seg_at(t0 + BLOCK - 1))
                if d == 0
                else (seg_at(t0 + BLOCK), seg_at(t0))
            )
            last = cum[BLOCK - 1 : BLOCK, :] if d == 0 else cum[0:1, :]
            lead_s[n] = jnp.where(seg_r == in_seg, jnp.exp(cum), 0.0)
            tail_s[n] = jnp.where(seg_r == out_seg, jnp.exp(last - cum), 0.0) * step
            same = jnp.where(in_seg == out_seg, 1.0, 0.0)
            fade_s[n, 0:1, :] = jnp.exp(last) * same
            bcj = bc[j * BLOCK : (j + 1) * BLOCK, :]
            b_only = jnp.where(low, bcj, 0.0).astype(BF16)
            c_low = pltpu.roll(bcj, HEAD_DIM, 1).astype(BF16)
            scores = lax.dot_general(
                c_low, b_only, (((1,), (1,)), ((), ())), preferred_element_type=F32
            )
            msc_s[n] = jnp.where(tri & (seg_r == seg_c), scores, 0.0)
            bt_s[n] = bcj.T[0:STATE, :].astype(BF16)
            cr_s[n] = c_low

    in1a = level1(0, d_a)
    in1b = level1(1, d_b)

    def local_pairs(lo, hi):
        @pl.loop(lo, hi)
        def _(p):
            lanes = lanes_of(p)
            shift = 128 - 2 * p
            head = core * (HEADS // 2) + 2 * p
            for d in range(2):
                skips = jnp.where(low1, skip_ref[d, head], skip_ref[d, head + 1])
                for j in range(2):
                    n = d * 2 + j
                    rows = slice(j * BLOCK, (j + 1) * BLOCK)
                    xt = xs[d, rows, lanes]
                    cums = pltpu.roll(cum_s[n], shift, 1)
                    ws = []
                    for hh in range(2):
                        h = pl.ds(2 * p + hh, 1)
                        gap = jnp.minimum(cums[:, hh : hh + 1] - cumt_s[n, h, :], 0.0)
                        ws.append((jnp.exp(gap) * msc_s[n] * stept_s[n, h, :]).astype(BF16))
                    xf = xt.astype(F32)
                    xl = jnp.where(low, xf, 0.0).astype(BF16)
                    xh = jnp.where(low, 0.0, xf).astype(BF16)
                    inner = jnp.dot(
                        jnp.concatenate(ws, axis=1),
                        jnp.concatenate([xl, xh], axis=0),
                        preferred_element_type=F32,
                    )
                    ys[d, rows, lanes] = inner + skips * xf

    def member(d, step, count):
        return d * (count - 1) + (1 - 2 * d) * step

    def level2(ph, d, copies):
        for c in copies:
            c.wait_recv()
        total = jnp.zeros((STATE, ql), F32)
        fade = jnp.ones((1, ql), F32)
        for step in range(zl):
            c = member(d, step, zl)
            f = rf1[d, c]
            total = f * total + r1[d, c].astype(F32)
            fade = fade * f
        gb[d, zh] = total.astype(BF16)
        gf[d, zh] = fade
        out = []
        for k in range(1, zh_n):
            for a, buf in enumerate((gb, gf)):
                c = remote(
                    buf.at[d, zh],
                    buf.at[d, zh],
                    g_ss.at[ph, k, a],
                    g_rs.at[ph, k, a],
                    zh_peers[k - 1],
                )
                c.start()
                sent.append(c)
                out.append(c)
        return out

    def level4(ph, d, state):
        for step in range(zh_n - 1):
            c = member(d, step, zh_n)
            before = (1 - 2 * d) * (zh - c) > 0
            longer = gf[d, c] * state + gb[d, c].astype(F32)
            state = jnp.where(before, longer, state)
        for step in range(zl):
            c = member(d, step, zl)
            o4[d, c] = state.astype(BF16)
            if step < zl - 1:
                state = rf1[d, c] * state + r1[d, c].astype(F32)
        out = []
        for k in range(1, zl):
            to = lax.rem(q + k, zl)
            c = remote(
                o4.at[d, to], sin.at[d, q], l_ss.at[ph, 0, k], l_rs.at[ph, 0, k], zl_peers[k - 1]
            )
            c.start()
            sent.append(c)
            out.append(c)
        sin[d, q] = o4[d, q]
        return out

    local_pairs(0, 4)
    in2a = level2(0, d_a, in1a)
    local_pairs(4, 7)
    in2b = level2(1, d_b, in1b)
    local_pairs(7, 8)
    for c in in2a:
        c.wait_recv()
    total = jnp.zeros((STATE, ql), F32)
    for step in range(zh_n):
        c = member(d_a, step, zh_n)
        total = gf[d_a, c] * total + gb[d_a, c].astype(F32)
    tb[...] = total.astype(BF16)
    in3 = remote(tb, tr, g_ss.at[0, 0, 0], g_rs.at[0, 0, 0], y_peer)
    in3.start()
    sent.append(in3)
    in4a = level4(0, d_a, jnp.zeros((STATE, ql), F32))
    for c in in2b:
        c.wait_recv()
    in3.wait_recv()
    in4b = level4(1, d_b, tr[...].astype(F32))

    row_q = lax.div(lax.broadcasted_iota(jnp.int32, (ql, ql), 0), HEAD_DIM)
    lane_q = lax.div(lax.broadcasted_iota(jnp.int32, (ql, ql), 1), HEAD_DIM)
    ones = jnp.where(row_q == lane_q, 1.0 / HEAD_DIM, 0.0).astype(BF16)

    def finish(quarter, d, last):
        lanes = pl.ds(pl.multiple_of(quarter * ql, ql), ql)
        wl = pl.ds(pl.multiple_of(core * HALF + quarter * ql, ql), ql)
        gains = jnp.where(d == 0, gain_ref[0:1, wl], gain_ref[1:2, wl])
        entering = sin[d, quarter]
        second = fb[d, 0:1, lanes] * entering.astype(F32) + lk[d, :, lanes]
        for j, state in ((d, entering), (1 - d, second.astype(BF16))):
            n = d * 2 + j
            rows = pl.ds(pl.multiple_of(j * BLOCK, BLOCK), BLOCK)
            carried = jnp.dot(cr_s[n, :, 0:STATE], state, preferred_element_type=F32)
            lead = pltpu.roll(lead_s[n], 128 - 2 * tq * quarter, 1)
            leads = jnp.concatenate(
                [
                    jnp.where(low, lead[:, 2 * t : 2 * t + 1], lead[:, 2 * t + 1 : 2 * t + 2])
                    for t in range(tq)
                ],
                axis=1,
            )
            yv = ys[d, rows, lanes] + leads * carried
            mean = jnp.dot((yv * yv).astype(BF16), ones, preferred_element_type=F32)
            res = yv * lax.rsqrt(mean + 1e-05) * gains
            if last:
                outb[quarter, j] = (res + ys[1 - d, rows, lanes]).astype(BF16)
            else:
                ys[d, rows, lanes] = res

    finish(q, d_a, False)
    for k in range(1, zl):
        in4a[k - 1].wait_recv()
        finish(lax.rem(q + zl - k, zl), d_a, False)
    outs = []
    for k in range(zl):
        quarter = lax.rem(q + zl - k, zl)
        if k > 0:
            in4b[k - 1].wait_recv()
        finish(quarter, d_b, True)
        cols = pl.ds(pl.multiple_of(core * HALF + quarter * ql, ql), ql)
        oc = remote(
            outb.at[quarter, 1 - core], out_ref.at[0, :, cols], o_ss.at[k], o_rs.at[k], partner
        )
        oc.start()
        own = pltpu.make_async_copy(
            outb.at[quarter, core], out_ref.at[0, :, cols], own_sem.at[k]
        )
        own.start()
        outs.append((oc, own))
    for oc, own in outs:
        own.wait()
        oc.wait()
    for c in sent:
        c.wait_send()


def solution(mesh):
    nx, ny, seqs = mesh.shape["fsdp"], mesh.shape["batch"], mesh.shape["seq"]
    nz = seqs // 4
    zl = 4 if nz % 4 == 0 and nz > 4 else 2
    zh_n = nz // zl
    ql = HALF // zl
    cfg = (nx, ny, nz, zl, zh_n, seqs)

    def on_device(hidden, in_weight, marks, cw, cb, dtb, dec, skip, gain):
        kb = in_weight.shape[0]
        vmem = pl.BlockSpec(memory_space=pltpu.VMEM)
        hbm = pl.BlockSpec(memory_space=pl.ANY)
        smem = pl.BlockSpec(memory_space=pltpu.SMEM)
        dma = pltpu.SemaphoreType.DMA
        return pl.pallas_call(
            functools.partial(kernel, cfg),
            out_shape=jax.ShapeDtypeStruct(hidden.shape, BF16),
            in_specs=[hbm, hbm, smem, vmem, vmem, vmem, vmem, smem, vmem],
            out_specs=hbm,
            scratch_shapes=[
                pltpu.VMEM((nx, ny, 3 * PART, kb), BF16),
                pltpu.VMEM((ROWS, INNER), BF16),
                pltpu.VMEM((ROWS, HALF + 256), F32),
                pltpu.VMEM((ROWS, 128), BF16),
                pltpu.VMEM((ROWS, 128), BF16),
                pltpu.VMEM((2, 2 * BLOCK, HALF), BF16),
                pltpu.VMEM((2, 2 * BLOCK, HALF), F32),
                pltpu.VMEM((2, STATE, HALF), F32),
                pltpu.VMEM((2, zl, STATE, ql), BF16),
                pltpu.VMEM((2, zl, 1, ql), F32),
                pltpu.VMEM((2, 8, HALF), F32),
                pltpu.VMEM((2, zl, STATE, ql), BF16),
                pltpu.VMEM((2, zl, 1, ql), F32),
                pltpu.VMEM((2, zh_n, STATE, ql), BF16),
                pltpu.VMEM((2, zh_n, 1, ql), F32),
                pltpu.VMEM((STATE, ql), BF16),
                pltpu.VMEM((STATE, ql), BF16),
                pltpu.VMEM((2, zl, STATE, ql), BF16),
                pltpu.VMEM((2, zl, STATE, ql), BF16),
                pltpu.VMEM((zl, 2, BLOCK, ql), BF16),
                pltpu.VMEM((8, 128), F32),
                pltpu.VMEM((4, 128, 128), F32),
                pltpu.VMEM((4, 128, 128), F32),
                pltpu.VMEM((4, 128, 128), F32),
                pltpu.VMEM((4, 128, 128), F32),
                pltpu.VMEM((4, 128, 128), F32),
                pltpu.VMEM((4, 128, 128), F32),
                pltpu.VMEM((4, STATE, 128), BF16),
                pltpu.VMEM((4, 128, 128), BF16),
                pltpu.VMEM((4, 8, 128), F32),
                dma((64,)),
                dma((64,)),
                dma((4,)),
                dma((4,)),
                dma((2, 4, 4)),
                dma((2, 4, 4)),
                dma((2, 3, 2)),
                dma((2, 3, 2)),
                dma((6,)),
                dma((4,)),
                dma((4,)),
                dma((4,)),
            ],
            compiler_params=pltpu.CompilerParams(
                collective_id=0, has_side_effects=True, vmem_limit_bytes=48 * 1024 * 1024
            ),
        )(hidden, in_weight.T, marks, cw, cb, dtb, dec, skip, gain)

    group = P(("fsdp", "batch"), "seq", None)
    rows = P(("fsdp", "batch"), None)
    return jax.shard_map(
        on_device,
        mesh=mesh,
        in_specs=(group, rows, rows, P(), P(), P(), P(), P(), P()),
        out_specs=group,
        check_vma=False,
    )
```

time: 91.4 us -> 84.5 us (0.925)
  Pallas kernels: 88.9 us -> 76.9 us
  local copies, waits for them, and re-layouts: 2.2 us -> 7.25 us
    pallas_call x1, Pallas kernels: 88.9 us -> 76.9 us  [on_device(): pl.pallas_call(functools.partial(kernel, cfg), out_shape=jax.ShapeDtypeSt...]
    unnamed x18 -> x19, local copies, waits for them, and re-layouts: 2.2 us -> 7.25 us
where the time goes in v2:
time: 84.5 us; the launch traced here: 84.1 us
  Pallas kernels  76.9 us (91%)
  local copies, waits for them, and re-layouts  7.25 us (9%)
    pallas_call x1, Pallas kernels, on_device(): pl.pallas_call(functools.partial(kernel, cfg), out_shape=jax.ShapeDtypeSt...  76.9 us
    unnamed x19, local copies, waits for them, and re-layouts  7.25 us

profile of v2, /device:TPU:1, one launch (start us, length us, event | category | flops | bytes accessed | tf_op | source)
XLA Modules:
  0.0 84.1 jit_solution(10435384783138942760)
XLA Ops:
  0.0 0.0 copy-start.5
  0.0 0.0 copy-start.8
  0.0 0.7 copy-done.5
  0.7 0.0 copy-done.8
  0.7 0.0 copy-start
  0.7 1.1 %copy-done = bf16[128,2208]{0,1:T(8,128)(2,1)S(1)} copy-done((bf16[128,2208]{0,1:T(8,128)(2,1)S(1)}, bf16[128,2208]{0,1:T(8,128)(2,1)}, u32[]{:S(2)}) %copy-start) | copy-done | bytes 565272
  1.7 0.0 copy-start.1
  1.7 1.0 %copy-done.1 = bf16[1,128,2048]{2,1,0:T(8,128)(2,1)S(1)} copy-done((bf16[1,128,2048]{2,1,0:T(8,128)(2,1)S(1)}, bf16[1,128,2048]{2,1,0:T(8,128)(2,1)}, u32[]{:S(2)}) %copy-start.1) | copy-done | bytes 524312
  2.8 0.0 copy-start.2
  2.8 0.9 %copy-done.2 = f32[2,4,2176]{2,1,0:T(4,128)S(1)} copy-done((f32[2,4,2176]{2,1,0:T(4,128)S(1)}, f32[2,4,2176]{2,1,0:T(4,128)}, u32[]{:S(2)}) %copy-start.2) | copy-done | bytes 69656
  3.7 0.0 copy-start.3
  3.7 0.7 copy-done.3
  4.4 0.0 copy-start.4
  4.4 0.7 copy-done.4
  5.1 0.0 copy-start.6
  5.1 0.7 copy-done.6
  5.8 0.0 copy-start.7
  5.8 0.7 copy-done.7
  6.5 76.9 %shard_map.91 = bf16[1,128,2048]{2,1,0:T(8,128)(2,1)S(1)} custom-call(bf16[1,128,2048]{2,1,0:T(8,128)(2,1)S(1)} %copy-done.1, bf16[2208,128]{1,0:T(8,128)(2,1)S(1)} %bitcast.1, s32[1,4]{1,0:T(1,128)S(1)} %copy-done.8, f32[2,4,2176]{2,1,0:T(4,128)S(1)} %copy-done.2, f32[2,2176]{1,0:T(2,128)S(1)} %copy-done.3, f32[2,32]{1,0:T(2,128)S(1)} %copy-done.5, ...), custom_call_target="tpu_custom_call" | custom-call | tf_op jit(solution)/shard_map/pallas_call | solution.py:647
  83.3 0.8 copy.11
Async XLA Ops:
  0.0 0.7 copy-start.5
  0.0 0.7 copy-start.8
  0.7 1.1 %copy-start = (bf16[128,2208]{0,1:T(8,128)(2,1)S(1)}, bf16[128,2208]{0,1:T(8,128)(2,1)}, u32[]{:S(2)}) copy-start(bf16[128,2208]{0,1:T(8,128)(2,1)} %param.10) | copy-start | bytes 1695748
  1.7 1.0 %copy-start.1 = (bf16[1,128,2048]{2,1,0:T(8,128)(2,1)S(1)}, bf16[1,128,2048]{2,1,0:T(8,128)(2,1)}, u32[]{:S(2)}) copy-start(bf16[1,128,2048]{2,1,0:T(8,128)(2,1)} %hid_ref.1) | copy-start | bytes 1572868
  2.8 0.9 %copy-start.2 = (f32[2,4,2176]{2,1,0:T(4,128)S(1)}, f32[2,4,2176]{2,1,0:T(4,128)}, u32[]{:S(2)}) copy-start(f32[2,4,2176]{2,1,0:T(4,128)} %cw_ref.1) | copy-start | bytes 208900
  3.7 0.7 copy-start.3
  4.4 0.7 copy-start.4
  5.1 0.7 copy-start.6
  5.8 0.7 copy-start.7

commit v3 on v2

--- a/solution.py
+++ b/solution.py
@@ -25,6 +25,14 @@
     cfg,
     hid_ref,
     w_ref,
+    marks_in,
+    cw_in,
+    cb_in,
+    dtb_in,
+    dec_in,
+    skip_in,
+    gain_in,
+    out_ref,
     marks_ref,
     cw_ref,
     cb_ref,
@@ -32,7 +40,6 @@
     dec_ref,
     skip_ref,
     gain_ref,
-    out_ref,
     wb,
     hidb,
     proj,
@@ -139,14 +146,22 @@
                 wb.at[0, 0, pl.ds(pl.multiple_of(dst, 32), count), :],
             )
         )
+    early = len(reads)
+    reads += [
+        (marks_in, marks_ref),
+        (cw_in, cw_ref),
+        (cb_in, cb_ref),
+        (dtb_in, dtb_ref),
+        (dec_in, dec_ref),
+        (skip_in, skip_ref),
+        (gain_in, gain_ref),
+    ]
     reads = [pltpu.make_async_copy(a, b, in_sem.at[k]) for k, (a, b) in enumerate(reads)]
     for c in reads:
         c.start()
     par[...] = jnp.zeros_like(par)
-    par[0:2, 0:HEADS] = dtb_ref[...]
-    par[2:4, 0:HEADS] = dec_ref[...]
     fade_s[...] = jnp.zeros_like(fade_s)
-    for c in reads:
+    for c in reads[1:early]:
         c.wait()
     pl.semaphore_wait(barrier, len(greet))
 
@@ -224,6 +239,11 @@
         sent.append(copy)
 
     def rows_wait():
+        reads[0].wait()
+        for c in reads[early:]:
+            c.wait()
+        par[0:2, 0:HEADS] = dtb_ref[...]
+        par[2:4, 0:HEADS] = dec_ref[...]
         pc.wait_recv()
         for side in range(2):
             rows = pl.ds((HALO + 2 * BLOCK) * side, HALO)
@@ -640,16 +660,21 @@
 
     def on_device(hidden, in_weight, marks, cw, cb, dtb, dec, skip, gain):
         kb = in_weight.shape[0]
-        vmem = pl.BlockSpec(memory_space=pltpu.VMEM)
         hbm = pl.BlockSpec(memory_space=pl.ANY)
-        smem = pl.BlockSpec(memory_space=pltpu.SMEM)
         dma = pltpu.SemaphoreType.DMA
         return pl.pallas_call(
             functools.partial(kernel, cfg),
             out_shape=jax.ShapeDtypeStruct(hidden.shape, BF16),
-            in_specs=[hbm, hbm, smem, vmem, vmem, vmem, vmem, smem, vmem],
+            in_specs=[hbm] * 9,
             out_specs=hbm,
             scratch_shapes=[
+                pltpu.SMEM(marks.shape, jnp.int32),
+                pltpu.VMEM(cw.shape, F32),
+                pltpu.VMEM(cb.shape, F32),
+                pltpu.VMEM(dtb.shape, F32),
+                pltpu.VMEM(dec.shape, F32),
+                pltpu.SMEM(skip.shape, F32),
+                pltpu.VMEM(gain.shape, F32),
                 pltpu.VMEM((nx, ny, 3 * PART, kb), BF16),
                 pltpu.VMEM((ROWS, INNER), BF16),
                 pltpu.VMEM((ROWS, HALF + 256), F32),
@@ -688,13 +713,13 @@
                 dma((2, 4, 4)),
                 dma((2, 3, 2)),
                 dma((2, 3, 2)),
-                dma((6,)),
+                dma((13,)),
                 dma((4,)),
                 dma((4,)),
                 dma((4,)),
             ],
             compiler_params=pltpu.CompilerParams(
-                collective_id=0, has_side_effects=True, vmem_limit_bytes=48 * 1024 * 1024
+                collective_id=0, has_side_effects=True, vmem_limit_bytes=67043328
             ),
         )(hidden, in_weight.T, marks, cw, cb, dtb, dec, skip, gain)
 

time: 84.5 us -> 78.2 us (0.925)
  local copies, waits for them, and re-layouts: 7.25 us -> 1.88 us
    unnamed x19 -> x1, local copies, waits for them, and re-layouts: 7.25 us -> 1.88 us
where the time goes in v3:
time: 78.2 us; the launch traced here: 78 us
  Pallas kernels  76.1 us (97%)
  local copies, waits for them, and re-layouts  1.88 us (2%)
    pallas_call x1, Pallas kernels, on_device(): pl.pallas_call(functools.partial(kernel, cfg), out_shape=jax.ShapeDtypeSt...  76.1 us
    unnamed x1, local copies, waits for them, and re-layouts  1.88 us

profile of v3, /device:TPU:1, one launch (start us, length us, event | category | flops | bytes accessed | tf_op | source)
XLA Modules:
  0.0 78.0 jit_solution(18428680727587174025)
XLA Ops:
  0.0 76.1 %shard_map.91 = bf16[1,128,2048]{2,1,0:T(8,128)(2,1)} custom-call(bf16[1,128,2048]{2,1,0:T(8,128)(2,1)} %hid_ref.1, bf16[2208,128]{1,0:T(8,128)(2,1)} %bitcast.1, s32[1,4]{1,0:T(1,128)} %marks_in.1, f32[2,4,2176]{2,1,0:T(4,128)} %cw_in.1, f32[2,2176]{1,0:T(2,128)} %cb_in.1, f32[2,32]{1,0:T(2,128)} %dtb_in.1, f32[2,32]{1,0:T(2,128)} %dec_in.1, ...), custom_call_target="tpu_custom_call" | custom-call | tf_op jit(solution)/shard_map/pallas_call | solution.py:665
  76.1 1.9 %copy.11 = bf16[1,128,2048]{2,1,0:T(8,128)(2,1)} copy(bf16[1,128,2048]{2,1,0:T(8,128)(2,1)} %shard_map.91) | data formatting | bytes 1048576

commit v4 on v3

--- a/solution.py
+++ b/solution.py
@@ -365,7 +365,8 @@
         for k in range(4):
             r0 = HALO - 3 + k if d == 0 else HALO + 3 - k
             total = total + cw_ref[d, k : k + 1, wlanes] * proj[pl.ds(r0, 2 * BLOCK), lanes]
-        return total * jax.nn.sigmoid(total)
+        half = 0.5 * total
+        return half + half * jnp.tanh(half)
 
     row_i = lax.broadcasted_iota(jnp.int32, (128, 128), 0)
     lane_i = lax.broadcasted_iota(jnp.int32, (128, 128), 1)
@@ -411,8 +412,11 @@
             ls[d, quarter, :, inner] = (fades[1] * ends[0] + ends[1]).astype(BF16)
             fs[d, quarter, :, inner] = fades[0] * fades[1]
 
+    def half_rows(ch):
+        return pl.ds(ch * (STATE // 2), STATE // 2)
+
     def level1(ph, d):
-        copies = []
+        copies = [[], []]
         for k in sorted(range(zl), key=lambda k: (k == 0, abs(k - zl // 2))):
             to = lax.rem(q + k, zl)
             summary(d, to)
@@ -420,17 +424,18 @@
                 r1[d, q] = ls[d, q]
                 rf1[d, q] = fs[d, q]
                 continue
-            for a, (src, dst) in enumerate(((ls, r1), (fs, rf1))):
+            for ch, src, dst in (
+                (0, fs.at[d, to], rf1.at[d, q]),
+                (0, ls.at[d, to, half_rows(0)], r1.at[d, q, half_rows(0)]),
+                (1, ls.at[d, to, half_rows(1)], r1.at[d, q, half_rows(1)]),
+            ):
+                a = len(copies[ch]) % 2 if ch == 0 else 0
                 c = remote(
-                    src.at[d, to],
-                    dst.at[d, q],
-                    l_ss.at[ph, k, a],
-                    l_rs.at[ph, k, a],
-                    zl_peers[k - 1],
+                    src, dst, l_ss.at[ph, ch, k, a], l_rs.at[ph, ch, k, a], zl_peers[k - 1]
                 )
                 c.start()
                 sent.append(c)
-                copies.append(c)
+                copies[ch].append(c)
         return copies
 
     d_a, d_b = yh, 1 - yh
@@ -522,76 +527,88 @@
     def member(d, step, count):
         return d * (count - 1) + (1 - 2 * d) * step
 
-    def level2(ph, d, copies):
-        for c in copies:
+    def level2(ph, d, copies, ch):
+        for c in copies[ch]:
             c.wait_recv()
-        total = jnp.zeros((STATE, ql), F32)
+        total = jnp.zeros((STATE // 2, ql), F32)
         fade = jnp.ones((1, ql), F32)
         for step in range(zl):
             c = member(d, step, zl)
             f = rf1[d, c]
-            total = f * total + r1[d, c].astype(F32)
+            total = f * total + r1[d, c, half_rows(ch)].astype(F32)
             fade = fade * f
-        gb[d, zh] = total.astype(BF16)
-        gf[d, zh] = fade
+        gb[d, zh, half_rows(ch)] = total.astype(BF16)
+        bufs = [gb.at[d, zh, half_rows(ch)]]
+        if ch == 0:
+            gf[d, zh] = fade
+            bufs.append(gf.at[d, zh])
         out = []
         for k in range(1, zh_n):
-            for a, buf in enumerate((gb, gf)):
+            for a, buf in enumerate(bufs):
                 c = remote(
-                    buf.at[d, zh],
-                    buf.at[d, zh],
-                    g_ss.at[ph, k, a],
-                    g_rs.at[ph, k, a],
-                    zh_peers[k - 1],
+                    buf, buf, g_ss.at[ph, ch, k, a], g_rs.at[ph, ch, k, a], zh_peers[k - 1]
                 )
                 c.start()
                 sent.append(c)
                 out.append(c)
         return out
 
-    def level4(ph, d, state):
+    def level4(ph, d, state, ch):
         for step in range(zh_n - 1):
             c = member(d, step, zh_n)
             before = (1 - 2 * d) * (zh - c) > 0
-            longer = gf[d, c] * state + gb[d, c].astype(F32)
+            longer = gf[d, c] * state + gb[d, c, half_rows(ch)].astype(F32)
             state = jnp.where(before, longer, state)
         for step in range(zl):
             c = member(d, step, zl)
-            o4[d, c] = state.astype(BF16)
+            o4[d, c, half_rows(ch)] = state.astype(BF16)
             if step < zl - 1:
-                state = rf1[d, c] * state + r1[d, c].astype(F32)
+                state = rf1[d, c] * state + r1[d, c, half_rows(ch)].astype(F32)
         out = []
         for k in range(1, zl):
             to = lax.rem(q + k, zl)
             c = remote(
-                o4.at[d, to], sin.at[d, q], l_ss.at[ph, 0, k], l_rs.at[ph, 0, k], zl_peers[k - 1]
+                o4.at[d, to, half_rows(ch)],
+                sin.at[d, q, half_rows(ch)],
+                l_ss.at[ph, ch, 0, k],
+                l_rs.at[ph, ch, 0, k],
+                zl_peers[k - 1],
             )
             c.start()
             sent.append(c)
             out.append(c)
-        sin[d, q] = o4[d, q]
+        sin[d, q, half_rows(ch)] = o4[d, q, half_rows(ch)]
         return out
 
-    local_pairs(0, 4)
-    in2a = level2(0, d_a, in1a)
-    local_pairs(4, 7)
-    in2b = level2(1, d_b, in1b)
+    local_pairs(0, 7)
+    in2a = [level2(0, d_a, in1a, ch) for ch in range(2)]
+    in2b = [level2(1, d_b, in1b, ch) for ch in range(2)]
     local_pairs(7, 8)
-    for c in in2a:
-        c.wait_recv()
-    total = jnp.zeros((STATE, ql), F32)
-    for step in range(zh_n):
-        c = member(d_a, step, zh_n)
-        total = gf[d_a, c] * total + gb[d_a, c].astype(F32)
-    tb[...] = total.astype(BF16)
-    in3 = remote(tb, tr, g_ss.at[0, 0, 0], g_rs.at[0, 0, 0], y_peer)
-    in3.start()
-    sent.append(in3)
-    in4a = level4(0, d_a, jnp.zeros((STATE, ql), F32))
-    for c in in2b:
-        c.wait_recv()
-    in3.wait_recv()
-    in4b = level4(1, d_b, tr[...].astype(F32))
+    in3, in4a, in4b = [], [], []
+    for ch in range(2):
+        for c in in2a[ch]:
+            c.wait_recv()
+        total = jnp.zeros((STATE // 2, ql), F32)
+        for step in range(zh_n):
+            c = member(d_a, step, zh_n)
+            total = gf[d_a, c] * total + gb[d_a, c, half_rows(ch)].astype(F32)
+        tb[half_rows(ch), :] = total.astype(BF16)
+        c = remote(
+            tb.at[half_rows(ch), :],
+            tr.at[half_rows(ch), :],
+            g_ss.at[0, ch, 0, 0],
+            g_rs.at[0, ch, 0, 0],
+            y_peer,
+        )
+        c.start()
+        sent.append(c)
+        in3.append(c)
+        in4a.append(level4(0, d_a, jnp.zeros((STATE // 2, ql), F32), ch))
+    for ch in range(2):
+        for c in in2b[ch]:
+            c.wait_recv()
+        in3[ch].wait_recv()
+        in4b.append(level4(1, d_b, tr[half_rows(ch), :].astype(F32), ch))
 
     row_q = lax.div(lax.broadcasted_iota(jnp.int32, (ql, ql), 0), HEAD_DIM)
     lane_q = lax.div(lax.broadcasted_iota(jnp.int32, (ql, ql), 1), HEAD_DIM)
@@ -625,13 +642,15 @@
 
     finish(q, d_a, False)
     for k in range(1, zl):
-        in4a[k - 1].wait_recv()
+        for ch in range(2):
+            in4a[ch][k - 1].wait_recv()
         finish(lax.rem(q + zl - k, zl), d_a, False)
     outs = []
     for k in range(zl):
         quarter = lax.rem(q + zl - k, zl)
         if k > 0:
-            in4b[k - 1].wait_recv()
+            for ch in range(2):
+                in4b[ch][k - 1].wait_recv()
         finish(quarter, d_b, True)
         cols = pl.ds(pl.multiple_of(core * HALF + quarter * ql, ql), ql)
         oc = remote(
@@ -709,10 +728,10 @@
                 dma((64,)),
                 dma((4,)),
                 dma((4,)),
-                dma((2, 4, 4)),
-                dma((2, 4, 4)),
-                dma((2, 3, 2)),
-                dma((2, 3, 2)),
+                dma((2, 2, 4, 4)),
+                dma((2, 2, 4, 4)),
+                dma((2, 2, 3, 2)),
+                dma((2, 2, 3, 2)),
                 dma((13,)),
                 dma((4,)),
                 dma((4,)),

time: 78.2 us -> 79.5 us (1.017)
  Pallas kernels: 76.1 us -> 77.4 us
    pallas_call x1, Pallas kernels: 76.1 us -> 77.4 us  [on_device(): pl.pallas_call(functools.partial(kernel, cfg), out_shape=jax.ShapeDtypeSt...]
where the time goes in v4:
time: 79.5 us; the launch traced here: 79.3 us
  Pallas kernels  77.4 us (97%)
  local copies, waits for them, and re-layouts  1.88 us (2%)
    pallas_call x1, Pallas kernels, on_device(): pl.pallas_call(functools.partial(kernel, cfg), out_shape=jax.ShapeDtypeSt...  77.4 us
    unnamed x1, local copies, waits for them, and re-layouts  1.88 us

profile of v4, /device:TPU:1, one launch (start us, length us, event | category | flops | bytes accessed | tf_op | source)
XLA Modules:
  0.0 79.3 jit_solution(13067018445713069504)
XLA Ops:
  0.0 77.4 %shard_map.91 = bf16[1,128,2048]{2,1,0:T(8,128)(2,1)} custom-call(bf16[1,128,2048]{2,1,0:T(8,128)(2,1)} %hid_ref.1, bf16[2208,128]{1,0:T(8,128)(2,1)} %bitcast.1, s32[1,4]{1,0:T(1,128)} %marks_in.1, f32[2,4,2176]{2,1,0:T(4,128)} %cw_in.1, f32[2,2176]{1,0:T(2,128)} %cb_in.1, f32[2,32]{1,0:T(2,128)} %dtb_in.1, f32[2,32]{1,0:T(2,128)} %dec_in.1, ...), custom_call_target="tpu_custom_call" | custom-call | tf_op jit(solution)/shard_map/pallas_call | solution.py:684
  77.4 1.9 %copy.11 = bf16[1,128,2048]{2,1,0:T(8,128)(2,1)} copy(bf16[1,128,2048]{2,1,0:T(8,128)(2,1)} %shard_map.91) | data formatting | bytes 1048576

commit v5 on v3

--- a/solution.py
+++ b/solution.py
@@ -251,6 +251,38 @@
                 hid_ref.at[0, 0:HALO, :], hidb.at[rows, :], h_ss.at[1], h_rs.at[1 + side], partner
             ).wait_recv()
 
+    def conv(d, lanes, wlanes):
+        total = jnp.broadcast_to(cb_ref[d : d + 1, wlanes], (2 * BLOCK, 128))
+        for k in range(4):
+            r0 = HALO - 3 + k if d == 0 else HALO + 3 - k
+            total = total + cw_ref[d, k : k + 1, wlanes] * proj[pl.ds(r0, 2 * BLOCK), lanes]
+        return total * jax.nn.sigmoid(total)
+
+    def lanes_of(p):
+        return pl.ds(pl.multiple_of(p * 128, 128), 128)
+
+    first_f = jnp.where(chip == 0, 0.0, 1.0)
+    last_f = jnp.where(chip == chips - 1, 0.0, 1.0)
+
+    def ends_off(lanes):
+        proj[0:HALO, lanes] = proj[0:HALO, lanes] * first_f
+        proj[HALO + 2 * BLOCK :, lanes] = proj[HALO + 2 * BLOCK :, lanes] * last_f
+
+    def convolve(u):
+        lanes = part_lanes[u]
+        proj[:, lanes] = proj[:, lanes].astype(BF16).astype(F32)
+        ends_off(lanes)
+
+        @pl.loop(0, PART // 128)
+        def _(i):
+            p = lax.rem(rot + (u + 1) % 3, 3) * (PART // 128) + i
+
+            @pl.when(p < HALF // 128)
+            def _():
+                wl = pl.ds(pl.multiple_of(core * HALF + p * 128, 128), 128)
+                for d in range(2):
+                    xs[d, :, lanes_of(p)] = conv(d, lanes_of(p), wl).astype(BF16)
+
     def project(slots, parts, first=False):
         left = []
         for i, j in slots:
@@ -329,44 +361,28 @@
                     if (i, j) != (0, 0):
                         zmsgs[(h, i, j)].wait_recv()
 
-        z_wait(order_k[0])
-        project(order_k[0], zz, True)
-        z_wait(order_k[1])
-        project(order_k[1], zz)
         for h in halves:
             w_wait(h, 3, 2)
         project(order_k[6], xy)
         for h in halves:
             w_wait(h, 2, 2)
         project(order_k[7], xy)
-        for slots in order_k[2:]:
+        convolve(0)
+        convolve(1)
+        for slots in order_k:
             z_wait(slots)
-            project(slots, zz)
+            project(slots, zz, slots is order_k[0])
     else:
         rows_wait()
         project(((0, 0),), (0, 1, 2), True)
+        convolve(0)
+        convolve(1)
 
     tile[...] = proj[:, HALF : HALF + 128].astype(BF16)
     swap_tile = remote(tile, other, h_ss.at[3], h_rs.at[3], partner)
     swap_tile.start()
     sent.append(swap_tile)
-    first_f = jnp.where(chip == 0, 0.0, 1.0)
-    last_f = jnp.where(chip == chips - 1, 0.0, 1.0)
-
-    def ends_off(lanes):
-        proj[0:HALO, lanes] = proj[0:HALO, lanes] * first_f
-        proj[HALO + 2 * BLOCK :, lanes] = proj[HALO + 2 * BLOCK :, lanes] * last_f
-
-    proj[:, 0:HALF] = proj[:, 0:HALF].astype(BF16).astype(F32)
-    ends_off(slice(0, HALF))
-
-    def conv(d, lanes, wlanes):
-        total = jnp.broadcast_to(cb_ref[d : d + 1, wlanes], (2 * BLOCK, 128))
-        for k in range(4):
-            r0 = HALO - 3 + k if d == 0 else HALO + 3 - k
-            total = total + cw_ref[d, k : k + 1, wlanes] * proj[pl.ds(r0, 2 * BLOCK), lanes]
-        return total * jax.nn.sigmoid(total)
-
+    convolve(2)
     row_i = lax.broadcasted_iota(jnp.int32, (128, 128), 0)
     lane_i = lax.broadcasted_iota(jnp.int32, (128, 128), 1)
     low = lane_i < HEAD_DIM
@@ -381,15 +397,6 @@
 
     def pair(value, mask):
         return jnp.where(mask, value[:, 0:1], value[:, 1:2])
-
-    def lanes_of(p):
-        return pl.ds(pl.multiple_of(p * 128, 128), 128)
-
-    @pl.loop(0, HALF // 128)
-    def _(p):
-        wl = pl.ds(pl.multiple_of(core * HALF + p * 128, 128), 128)
-        for d in range(2):
-            xs[d, :, lanes_of(p)] = conv(d, lanes_of(p), wl).astype(BF16)
 
     def summary(d, quarter):
         fades_d = [fade_s[d * 2 + d], fade_s[d + 1]]

time: 78.2 us -> 78 us (level)
  the two profiles are of different devices: /device:TPU:1 before, /device:TPU:5 now
where the time goes in v5:
time: 78 us; the launch traced here: 77.9 us
  Pallas kernels  76 us (97%)
  local copies, waits for them, and re-layouts  1.88 us (2%)
    pallas_call x1, Pallas kernels, on_device(): pl.pallas_call(functools.partial(kernel, cfg), out_shape=jax.ShapeDtypeSt...  76 us
    unnamed x1, local copies, waits for them, and re-layouts  1.88 us

profile of v5, /device:TPU:5, one launch (start us, length us, event | category | flops | bytes accessed | tf_op | source)
XLA Modules:
  0.0 77.9 jit_solution(8370204505376952860)
XLA Ops:
  0.0 76.0 %shard_map.91 = bf16[1,128,2048]{2,1,0:T(8,128)(2,1)} custom-call(bf16[1,128,2048]{2,1,0:T(8,128)(2,1)} %hid_ref.1, bf16[2208,128]{1,0:T(8,128)(2,1)} %bitcast.1, s32[1,4]{1,0:T(1,128)} %marks_in.1, f32[2,4,2176]{2,1,0:T(4,128)} %cw_in.1, f32[2,2176]{1,0:T(2,128)} %cb_in.1, f32[2,32]{1,0:T(2,128)} %dtb_in.1, f32[2,32]{1,0:T(2,128)} %dec_in.1, ...), custom_call_target="tpu_custom_call" | custom-call | tf_op jit(solution)/shard_map/pallas_call | solution.py:672
  76.0 1.9 %copy.11 = bf16[1,128,2048]{2,1,0:T(8,128)(2,1)} copy(bf16[1,128,2048]{2,1,0:T(8,128)(2,1)} %shard_map.91) | data formatting | bytes 1048576

commit v6 on v5

--- a/solution.py
+++ b/solution.py
@@ -579,11 +579,10 @@
         sin[d, q] = o4[d, q]
         return out
 
-    local_pairs(0, 4)
+    local_pairs(0, 5)
     in2a = level2(0, d_a, in1a)
-    local_pairs(4, 7)
     in2b = level2(1, d_b, in1b)
-    local_pairs(7, 8)
+    local_pairs(5, 8)
     for c in in2a:
         c.wait_recv()
     total = jnp.zeros((STATE, ql), F32)

time: 78 us -> 77.4 us (level)
  the two profiles are of different devices: /device:TPU:5 before, /device:TPU:1 now
where the time goes in v6:
time: 77.4 us; the launch traced here: 77 us
  Pallas kernels  75.1 us (97%)
  local copies, waits for them, and re-layouts  1.88 us (2%)
    pallas_call x1, Pallas kernels, on_device(): pl.pallas_call(functools.partial(kernel, cfg), out_shape=jax.ShapeDtypeSt...  75.1 us
    unnamed x1, local copies, waits for them, and re-layouts  1.88 us

profile of v6, /device:TPU:1, one launch (start us, length us, event | category | flops | bytes accessed | tf_op | source)
XLA Modules:
  0.0 77.0 jit_solution(6305514616905809892)
XLA Ops:
  0.0 75.1 %shard_map.91 = bf16[1,128,2048]{2,1,0:T(8,128)(2,1)} custom-call(bf16[1,128,2048]{2,1,0:T(8,128)(2,1)} %hid_ref.1, bf16[2208,128]{1,0:T(8,128)(2,1)} %bitcast.1, s32[1,4]{1,0:T(1,128)} %marks_in.1, f32[2,4,2176]{2,1,0:T(4,128)} %cw_in.1, f32[2,2176]{1,0:T(2,128)} %cb_in.1, f32[2,32]{1,0:T(2,128)} %dtb_in.1, f32[2,32]{1,0:T(2,128)} %dec_in.1, ...), custom_call_target="tpu_custom_call" | custom-call | tf_op jit(solution)/shard_map/pallas_call | solution.py:671
  75.2 1.9 %copy.11 = bf16[1,128,2048]{2,1,0:T(8,128)(2,1)} copy(bf16[1,128,2048]{2,1,0:T(8,128)(2,1)} %shard_map.91) | data formatting | bytes 1048576
